TPU v7x, 32 devices: a whole 2x2x4 slice. The times are simulated.
32 devices in a mesh: seqa: 4 (over y, x), seqb: 8 (over z, core).
Axes of the slice: x: 2, y: 2, z: 4, core: 2. Of those that a mesh axis runs over, the one named last changes fastest.
Arguments:
- query_rows: bfloat16 [8192, 1024], P(('seqa', 'seqb')), may hold values from -256 to 256
- key_rows: bfloat16 [8192, 1024], P(('seqa', 'seqb')), may hold values from -16 to 16
- value_rows: bfloat16 [8192, 1024], P(('seqa', 'seqb')), may hold values from -16 to 16
Outputs:
- attended: bfloat16 [8192, 1024], P(('seqa', 'seqb'))
All inputs are finite; a program needn't handle non-finite values.
Results may differ from a plain program's by a relative error of at most 0.0027.
Values may be sent and summed in bfloat16 or wider, within the bound.
No kernel may reach another device: no remote copies, remote signals or barrier semaphores. Data moves between devices by JAX's collectives and lax.ppermute only.
A program may use at most 64 MiB of HBM per device.

v0:
```python
import functools

import jax
import jax.numpy as jnp
from jax import lax
from jax.experimental import pallas as pl
from jax.experimental.pallas import tpu as pltpu
from jax.sharding import PartitionSpec as P

HEADS = 8
HEAD_DIM = 128
HALF_WIN = 256
POOL = 4
CHIPS_ONE = 4
COLUMNS_THREE = 4
AXES = ("seqa", "seqb")
NEG = -1e30
EXP2_SCALE = 1.4426950408889634 / HEAD_DIM**0.5
VMEM_LIMIT = 24 << 20
POOL_LIMIT = 67043328 - (7 << 18)


def pool_rows(rows):
    count = rows.shape[0]
    groups = lax.broadcasted_iota(jnp.int32, (count // POOL, count), 1) // POOL
    owner = lax.broadcasted_iota(jnp.int32, (count // POOL, count), 0)
    mean = jnp.where(groups == owner, 1.0 / POOL, 0.0).astype(jnp.bfloat16)
    return jnp.dot(mean, rows, preferred_element_type=jnp.float32).astype(jnp.bfloat16)


def pool_kernel(k_ref, v_ref, one_ref, three_ref, rows_ref, sem):
    copies = [
        pltpu.make_async_copy(rows, rows_ref.at[side], sem.at[side])
        for side, rows in enumerate((k_ref, v_ref))
    ]
    for copy in copies:
        copy.start()
    for side, copy in enumerate(copies):
        copy.wait()
        one = pool_rows(rows_ref[side])
        one_ref[side] = one
        three_ref[side] = pool_rows(pool_rows(one))


def pool_call(key_rows, value_rows):
    rows, width = key_rows.shape
    shapes = [(2, rows // POOL**level, width) for level in (1, 3)]
    return pl.pallas_call(
        pool_kernel,
        in_specs=[pl.BlockSpec(memory_space=pltpu.HBM)] * 2,
        out_specs=[pl.BlockSpec(memory_space=pltpu.VMEM)] * 2,
        out_shape=[jax.ShapeDtypeStruct(shape, jnp.bfloat16) for shape in shapes],
        scratch_shapes=[
            pltpu.VMEM((2, rows, width), jnp.bfloat16),
            pltpu.SemaphoreType.DMA((2,)),
        ],
        name="pool_own",
        compiler_params=pltpu.CompilerParams(vmem_limit_bytes=POOL_LIMIT),
        cost_estimate=pl.CostEstimate(
            flops=4 * rows * rows * width // POOL, bytes_accessed=5 * rows * width, transcendentals=0
        ),
    )(key_rows, value_rows)


def lift_kernel(three_ref, other_ref, next_ref, far_ref, out_ref):
    count = three_ref.shape[1]
    for side in range(2):
        out_ref[side, pl.ds(0, count), :] = three_ref[side]
        out_ref[side, pl.ds(count, count), :] = other_ref[side]
        for slot, ref in enumerate((next_ref, far_ref)):
            out_ref[side, pl.ds((2 + slot) * count, count), :] = pool_rows(pool_rows(ref[side]))


def lift_call(own_three, other_three, one_next, one_far):
    _, count, width = own_three.shape
    return pl.pallas_call(
        lift_kernel,
        in_specs=[pl.BlockSpec(memory_space=pltpu.VMEM)] * 4,
        out_specs=pl.BlockSpec(memory_space=pltpu.VMEM),
        out_shape=jax.ShapeDtypeStruct((2, 4 * count, width), jnp.bfloat16),
        name="lift",
        compiler_params=pltpu.CompilerParams(vmem_limit_bytes=VMEM_LIMIT),
        cost_estimate=pl.CostEstimate(
            flops=16 * 64 * 16 * width, bytes_accessed=1200 * width, transcendentals=0
        ),
    )(own_three, other_three, one_next, one_far)


def triangle(shape, below):
    column = lax.broadcasted_iota(jnp.int32, shape, 0)
    row = lax.broadcasted_iota(jnp.int32, shape, 1)
    gap = column - row
    return jnp.where(jnp.where(below, gap, -1 - gap) < 0, 0.0, NEG)


def key_scores(keys, queries):
    return EXP2_SCALE * lax.dot_general(
        keys, queries, (((1,), (1,)), ((), ())), preferred_element_type=jnp.float32
    )


def stage_kernel(plan, first, *refs):
    refs = list(refs)
    flags_ref = refs.pop(0)
    q_ref = refs.pop(0)
    inputs = [refs.pop(0) for _, count in plan for _ in range(count)]
    if not first:
        top_in, sum_in, acc_in = refs.pop(0), refs.pop(0), refs.pop(0)
    top_out, sum_out, acc_out = refs.pop(0), refs.pop(0), refs.pop(0)
    expo_out = refs.pop(0) if any(kind == "across" for kind, _ in plan) else None
    far_ref = refs.pop(0)
    bias_ref = refs.pop(0)
    tok = q_ref.shape[0]
    lower_core = flags_ref[0] == 0
    middle = flags_ref[2] != 0
    whole = []
    place = 0
    for kind, count in plan:
        parts = [inputs.pop(0) for _ in range(count)]
        if kind in ("own", "partner", "across"):
            whole.append((parts, kind))
        if kind == "partner":
            bias_ref[...] = triangle((tok, tok), lower_core)
        if kind == "across":
            valid = jnp.where(flags_ref[1] != 0, 0.0, NEG)
            bias_ref[...] = triangle((tok, tok), jnp.logical_not(lower_core)) + valid
        if kind in ("own", "across"):
            continue
        for side in range(2):
            at = place
            if kind == "partner":
                rows = pool_rows(parts[side][...])
            elif kind == "pick":
                rows = jnp.where(middle, parts[0][side], parts[1][side])
            else:
                rows = parts[0][side]
            far_ref[side, pl.ds(at, rows.shape[0]), :] = rows
            at += rows.shape[0]
            if kind != "far":
                lower = pool_rows(rows)
                far_ref[side, pl.ds(at, lower.shape[0]), :] = lower
                at += lower.shape[0]
        place = at
    cols = [pl.ds(head * HEAD_DIM, HEAD_DIM) for head in range(HEADS)]
    scores = []
    for head in range(HEADS):
        query = q_ref[:, cols[head]]
        pieces = []
        for parts, kind in whole:
            piece = key_scores(parts[0][:, cols[head]], query)
            pieces.append(piece if kind == "own" else piece + bias_ref[...])
        pieces.append(key_scores(far_ref[0, pl.ds(0, place), cols[head]], query))
        scores.append(pieces)
    highest, keep = [], []
    for head in range(HEADS):
        top = functools.reduce(
            jnp.maximum, [jnp.max(piece, axis=0, keepdims=True) for piece in scores[head]]
        )
        if not first:
            before = top_in[pl.ds(head, 1), :]
            top = jnp.maximum(top, before)
            keep.append(jnp.exp2(before - top))
        highest.append(top)
    expos, totals = [], []
    for head in range(HEADS):
        expos.append([jnp.exp2(piece - highest[head]) for piece in scores[head]])
        total = sum(jnp.sum(piece, axis=0, keepdims=True) for piece in expos[head])
        if not first:
            total = total + sum_in[pl.ds(head, 1), :] * keep[head]
        totals.append(total)
    for head in range(HEADS):
        mixed = 0.0
        for (parts, kind), expo in zip(whole, expos[head]):
            if kind == "across":
                expo_out[pl.ds(head * tok, tok), :] = expo.astype(jnp.bfloat16)
            else:
                mixed = mixed + weighted(parts[1][:, cols[head]], expo.astype(jnp.bfloat16))
        mixed = mixed + weighted(
            far_ref[1, pl.ds(0, place), cols[head]], expos[head][-1].astype(jnp.bfloat16)
        )
        if not first:
            mixed = mixed + acc_in[cols[head], :] * keep[head]
        acc_out[cols[head], :] = mixed
        top_out[pl.ds(head, 1), :] = highest[head]
        sum_out[pl.ds(head, 1), :] = totals[head]


def weighted(values, expo):
    return lax.dot_general(
        values, expo, (((0,), (0,)), ((), ())), preferred_element_type=jnp.float32
    )


def far_count(kind, parts):
    if kind in ("own", "across"):
        return 0
    if kind == "partner":
        rows = parts[0].shape[0] // POOL
    else:
        rows = parts[0].shape[1]
    return rows if kind == "far" else rows + rows // POOL


def stage(flags, queries, inputs, state=None):
    tok, width = queries.shape
    plan = [(kind, len(arrays)) for kind, *arrays in inputs]
    arrays = [array for _, *group in inputs for array in group]
    far = sum(far_count(kind, group) for kind, *group in inputs)
    near = tok * sum(kind in ("own", "partner", "across") for kind, *_ in inputs)
    vmem = pl.BlockSpec(memory_space=pltpu.VMEM)
    operands = [flags, queries, *arrays, *(state or ())]
    stat = jax.ShapeDtypeStruct((HEADS, tok), jnp.float32)
    out_shape = [stat, stat, jax.ShapeDtypeStruct((width, tok), jnp.float32)]
    if any(kind == "across" for kind, _ in plan):
        out_shape.append(jax.ShapeDtypeStruct((HEADS * tok, tok), jnp.bfloat16))
    return pl.pallas_call(
        functools.partial(stage_kernel, plan, state is None),
        out_shape=out_shape,
        in_specs=[pl.BlockSpec(memory_space=pltpu.SMEM)] + [vmem] * (len(operands) - 1),
        out_specs=[vmem] * len(out_shape),
        scratch_shapes=[
            pltpu.VMEM((2, far, width), jnp.bfloat16),
            pltpu.VMEM((tok, tok), jnp.float32),
        ],
        compiler_params=pltpu.CompilerParams(vmem_limit_bytes=VMEM_LIMIT),
        cost_estimate=pl.CostEstimate(
            flops=4 * tok * width * (far + near),
            bytes_accessed=sum(a.size * a.dtype.itemsize for a in operands),
            transcendentals=tok * HEADS * (far + near),
        ),
    )(*operands)


def finish_kernel(value_ref, expo_ref, sum_ref, acc_ref, out_ref):
    tok = out_ref.shape[0]
    for head in range(HEADS):
        cols = pl.ds(head * HEAD_DIM, HEAD_DIM)
        mixed = weighted(value_ref[:, cols], expo_ref[pl.ds(head * tok, tok), :]) + acc_ref[cols, :]
        mixed = mixed * (1.0 / sum_ref[pl.ds(head, 1), :])
        out_ref[:, cols] = mixed.T.astype(jnp.bfloat16)


def finish(values, expo, total, mixed):
    tok, width = values.shape
    return pl.pallas_call(
        finish_kernel,
        out_shape=jax.ShapeDtypeStruct((tok, width), jnp.bfloat16),
        in_specs=[pl.BlockSpec(memory_space=pltpu.VMEM)] * 4,
        out_specs=pl.BlockSpec(memory_space=pltpu.VMEM),
        name="finish",
        compiler_params=pltpu.CompilerParams(vmem_limit_bytes=VMEM_LIMIT),
        cost_estimate=pl.CostEstimate(
            flops=2 * tok * tok * width, bytes_accessed=10 * tok * width, transcendentals=0
        ),
    )(values, expo, total, mixed)


def swap(x, axis, mask):
    return lax.ppermute(x, axis, [(i, i ^ mask) for i in range(lax.axis_size(axis))])


def spread(x, axis, low, high):
    while low < high:
        x = jnp.concatenate([x, swap(x, axis, low)], axis=1)
        low *= 2
    return x


def pooled_means(stacked):
    count = stacked.shape[1] // POOL
    split = stacked.astype(jnp.float32).reshape(2, count, POOL, stacked.shape[2])
    return split.mean(axis=2).astype(jnp.bfloat16)


def attend(query_rows, key_rows, value_rows):
    tok = query_rows.shape[0]
    assert tok == HALF_WIN
    wide, tall = lax.axis_size("seqb"), lax.axis_size("seqa")
    count = tall * wide
    group = 2 * CHIPS_ONE
    inner = lax.axis_index("seqb")
    place = lax.axis_index("seqa") * wide + inner
    core = inner & 1
    valid = jnp.where(core == 0, place > 0, place < count - 1)
    chip = (inner >> 1) & (CHIPS_ONE - 1)
    middle = (chip == 1) | (chip == 2)
    flags = jnp.stack([flag.astype(jnp.int32) for flag in (core, valid, middle)])
    bounds = [(i, i + 1) for i in range(1, count - 1, 2)]
    bounds += [(j, i) for i, j in bounds]
    own_one, own_three = pool_call(key_rows, value_rows)

    one_far = swap(own_one, "seqb", group - 2)
    one_next = swap(own_one, "seqb", 2)
    other_three = swap(own_three, "seqb", 4)
    chips = [(i, i // 2 % CHIPS_ONE) for i in range(wide)]
    one_end = lax.ppermute(own_one, "seqb", [(i, i ^ 4) for i, chip in chips if chip in (0, 3)])
    across_keys = lax.ppermute(key_rows, AXES, bounds)
    across_values = lax.ppermute(value_rows, AXES, bounds)
    partner = [swap(key_rows, "seqb", 1), swap(value_rows, "seqb", 1)]
    near_plan = [("own", key_rows, value_rows), ("one", own_one), ("partner", *partner)]
    state = stage(flags, query_rows, near_plan)
    one_mid = lax.ppermute(one_far, "seqb", [(i, i ^ 2) for i, chip in chips if chip in (1, 2)])
    three = lift_call(own_three, other_three, one_next, one_far)
    three = spread(three, "seqb", group, wide)
    three = spread(three, "seqa", 1, COLUMNS_THREE)
    far = [
        ("one", one_next),
        ("one", swap(one_next, "seqb", 1)),
        ("one", one_far),
        ("one", swap(one_far, "seqb", 1)),
    ]
    state = stage(flags, query_rows, far, state)
    wider = [
        ("pick", one_end, one_mid),
        ("pick", swap(one_end, "seqb", 1), swap(one_mid, "seqb", 1)),
        ("three", three),
        ("three", swap(three, "seqb", 1)),
    ]
    if wide > group:
        two = pooled_means(own_one)
        others = spread(two, "seqb", group, wide)[:, two.shape[1] :]
        wider.append(("far", spread(others, "seqb", 1, group)))
    if tall > COLUMNS_THREE:
        four = pooled_means(own_three)
        others = spread(four, "seqa", COLUMNS_THREE, tall)[:, four.shape[1] :]
        others = spread(others, "seqa", 1, COLUMNS_THREE)
        wider.append(("far", spread(others, "seqb", 1, wide)))
    _, total, mixed, expo = stage(flags, query_rows, wider + [("across", across_keys)], state)
    return finish(across_values, expo, total, mixed)


def solution(mesh):
    return jax.shard_map(
        attend,
        mesh=mesh,
        in_specs=(P(AXES, None), P(AXES, None), P(AXES, None)),
        out_specs=P(AXES, None),
        check_vma=False,
    )
```

profile of v0, /device:TPU:1, one launch (start us, length us, event | category | flops | bytes accessed | tf_op | source)
XLA Modules:
  0.0 64.6 jit_solution(6484141190246188702)
XLA Ops:
  0.0 2.6 %pool_own.1 = (bf16[2,64,1024]{2,1,0:T(8,128)(2,1)}, bf16[2,4,1024]{2,1,0:T(4,128)(2,1)}) custom-call(bf16[256,1024]{1,0:T(8,128)(2,1)} %refs_2_.1, bf16[256,1024]{1,0:T(8,128)(2,1)} %refs_3_.1), custom_call_target="tpu_custom_call" | custom-call | flops 67108864 | bytes 1310720 | tf_op jit(solution)/shard_map/pool_own/pallas_call | solution.py:48
  2.6 4.2 %collective-permute-start.2 = (bf16[2,64,1024]{2,1,0:T(8,128)(2,1)}, bf16[2,64,1024]{2,1,0:T(8,128)(2,1)S(1)}, u32[]{:S(2)}, u32[]{:S(2)}) collective-permute-start(bf16[2,64,1024]{2,1,0:T(8,128)(2,1)} %get-tuple-element.16.refs_4_), channel_id=1, source_target_pairs={{0,6},{1,7},{2,4},{3,5},{4,2},{5,3},{6,0},{7,1},{8,14},{9,15},{10,... | collective-permute-start | bytes 786440 | tf_op jit(solution)/shard_map/ppermute | solution.py:259
  6.9 1.0 %collective-permute-start.14 = (bf16[256,1024]{1,0:T(8,128)(2,1)S(1)}, bf16[256,1024]{1,0:T(8,128)(2,1)S(1)}, u32[]{:S(2)}, u32[]{:S(2)}) collective-permute-start(bf16[256,1024]{1,0:T(8,128)(2,1)S(1)} %copy-done.1), channel_id=1, source_target_pairs={{0,1},{1,0},{2,3},{3,2},{4,5},{5,4},{6,7},{7,6},{8,9},{9,8},{10,11... | collective-permute-start | bytes 1572872 | tf_op jit(solution)/shard_map/ppermute | solution.py:259
  8.3 9.9 %collective-permute-done.6.other_ref = bf16[2,4,1024]{2,1,0:T(4,128)(2,1)S(1)} collective-permute-done((bf16[2,4,1024]{2,1,0:T(4,128)(2,1)}, bf16[2,4,1024]{2,1,0:T(4,128)(2,1)S(1)}, u32[]{:S(2)}, u32[]{:S(2)}) %collective-permute-start.6) | collective-permute-done | bytes 16416 | tf_op jit(solution)/shard_map/ppermute | solution.py:259
  18.1 1.8 %collective-permute-done.7.next_ref.refs_2_ = bf16[2,64,1024]{2,1,0:T(8,128)(2,1)S(1)} collective-permute-done((bf16[2,64,1024]{2,1,0:T(8,128)(2,1)}, bf16[2,64,1024]{2,1,0:T(8,128)(2,1)S(1)}, u32[]{:S(2)}, u32[]{:S(2)}) %collective-permute-start.7) | collective-permute-done | bytes 262176 | tf_op jit(solution)/shard_map/ppermute | solution.py:259
  19.9 0.7 %copy-done.9 = bf16[2,4,1024]{2,1,0:T(4,128)(2,1)S(1)} copy-done((bf16[2,4,1024]{2,1,0:T(4,128)(2,1)S(1)}, bf16[2,4,1024]{2,1,0:T(4,128)(2,1)}, u32[]{:S(2)}) %copy-start.9) | copy-done | bytes 16408
  20.6 0.7 %lift.1 = bf16[2,16,1024]{2,1,0:T(8,128)(2,1)S(1)} custom-call(bf16[2,4,1024]{2,1,0:T(4,128)(2,1)S(1)} %copy-done.9, bf16[2,4,1024]{2,1,0:T(4,128)(2,1)S(1)} %collective-permute-done.6.other_ref, bf16[2,64,1024]{2,1,0:T(8,128)(2,1)S(1)} %collective-permute-done.7.next_ref.refs_2_, bf16[2,64,1024]{2,1,0:T(8,128)(2,1)S(1)} %collective-permute-done.2.far_ref.refs_4_), custom_call_target="tpu_custom_call" | custom-call | flops 16777216 | bytes 1228800 | tf_op jit(solution)/shard_map/lift/pallas_call | solution.py:76
  21.3 1.2 %collective-permute-start.8 = (bf16[2,16,1024]{2,1,0:T(8,128)(2,1)S(1)}, bf16[2,16,1024]{2,1,0:T(8,128)(2,1)S(1)}, u32[]{:S(2)}, u32[]{:S(2)}) collective-permute-start(bf16[2,16,1024]{2,1,0:T(8,128)(2,1)S(1)} %lift.1), channel_id=1, source_target_pairs={{0,8},{8,0},{16,24},{24,16},{1,9},{9,1},{17,25},{25,17},{2,10},{10... | collective-permute-start | bytes 196616 | tf_op jit(solution)/shard_map/ppermute | solution.py:259
  22.5 3.6 %collective-permute-start.1 = (bf16[2,64,1024]{2,1,0:T(8,128)(2,1)S(1)}, bf16[2,64,1024]{2,1,0:T(8,128)(2,1)}, u32[]{:S(2)}, u32[]{:S(2)}) collective-permute-start(bf16[2,64,1024]{2,1,0:T(8,128)(2,1)S(1)} %copy-done.3), channel_id=1, source_target_pairs={{0,4},{1,5},{6,2},{7,3},{8,12},{9,13},{14,10},{15,11},{16,20},{17,... | collective-permute-start | bytes 786440 | tf_op jit(solution)/shard_map/ppermute | solution.py:296
  26.2 1.3 %collective-permute-start.9 = (bf16[2,32,1024]{2,1,0:T(8,128)(2,1)S(1)}, bf16[2,32,1024]{2,1,0:T(8,128)(2,1)S(1)}, u32[]{:S(2)}, u32[]{:S(2)}) collective-permute-start(bf16[2,32,1024]{2,1,0:T(8,128)(2,1)S(1)} %pad_maximum_fusion.1), channel_id=1, source_target_pairs={{0,16},{8,24},{16,0},{24,8},{1,17},{9,25},{17,1},{25,9},{2,18},{10... | collective-permute-start | bytes 393224 | tf_op jit(solution)/shard_map/ppermute | solution.py:259
  27.5 3.2 %collective-permute-start.11 = (bf16[256,1024]{1,0:T(8,128)(2,1)S(1)}, bf16[256,1024]{1,0:T(8,128)(2,1)}, u32[]{:S(2)}, u32[]{:S(2)}) collective-permute-start(bf16[256,1024]{1,0:T(8,128)(2,1)S(1)} %copy-done.1), channel_id=1, source_target_pairs={{1,2},{3,4},{5,6},{7,8},{9,10},{11,12},{13,14},{15,16},{17,18},{19... | collective-permute-start | bytes 1572872 | tf_op jit(solution)/shard_map/ppermute | solution.py:297
  30.7 1.6 %collective-permute-start.13 = (bf16[2,64,1024]{2,1,0:T(8,128)(2,1)S(1)}, bf16[2,64,1024]{2,1,0:T(8,128)(2,1)S(1)}, u32[]{:S(2)}, u32[]{:S(2)}) collective-permute-start(bf16[2,64,1024]{2,1,0:T(8,128)(2,1)S(1)} %collective-permute-done.2.far_ref.refs_4_), channel_id=1, source_target_pairs={{0,1},{1,0},{2,3},{3,2},{4,5},{5,4},{6,7},{7,6},{8,9},{9,8},{10,11... | collective-permute-start | bytes 786440 | tf_op jit(solution)/shard_map/ppermute | solution.py:259
  32.3 1.2 %collective-permute-start.12 = (bf16[2,64,1024]{2,1,0:T(8,128)(2,1)S(1)}, bf16[2,64,1024]{2,1,0:T(8,128)(2,1)S(1)}, u32[]{:S(2)}, u32[]{:S(2)}) collective-permute-start(bf16[2,64,1024]{2,1,0:T(8,128)(2,1)S(1)} %collective-permute-done.7.next_ref.refs_2_), channel_id=1, source_target_pairs={{0,1},{1,0},{2,3},{3,2},{4,5},{5,4},{6,7},{7,6},{8,9},{9,8},{10,11... | collective-permute-start | bytes 786440 | tf_op jit(solution)/shard_map/ppermute | solution.py:259
  33.5 1.3 %collective-permute-start.3 = (bf16[2,64,1024]{2,1,0:T(8,128)(2,1)S(1)}, bf16[2,64,1024]{2,1,0:T(8,128)(2,1)}, u32[]{:S(2)}, u32[]{:S(2)}) collective-permute-start(bf16[2,64,1024]{2,1,0:T(8,128)(2,1)S(1)} %collective-permute-done.2.far_ref.refs_4_), channel_id=1, source_target_pairs={{2,0},{3,1},{4,6},{5,7},{10,8},{11,9},{12,14},{13,15},{18,16},{19,... | collective-permute-start | bytes 786440 | tf_op jit(solution)/shard_map/ppermute | solution.py:302
  34.8 4.8 %collective-permute-start = (bf16[256,1024]{1,0:T(8,128)(2,1)S(1)}, bf16[256,1024]{1,0:T(8,128)(2,1)}, u32[]{:S(2)}, u32[]{:S(2)}) collective-permute-start(bf16[256,1024]{1,0:T(8,128)(2,1)S(1)} %copy-done.2), channel_id=1, source_target_pairs={{1,2},{3,4},{5,6},{7,8},{9,10},{11,12},{13,14},{15,16},{17,18},{19... | collective-permute-start | bytes 1572872 | tf_op jit(solution)/shard_map/ppermute | solution.py:298
  39.7 0.7 %copy-done.5 = bf16[2,64,1024]{2,1,0:T(8,128)(2,1)} copy-done((bf16[2,64,1024]{2,1,0:T(8,128)(2,1)}, bf16[2,64,1024]{2,1,0:T(8,128)(2,1)S(1)}, u32[]{:S(2)}) %copy-start.5) | copy-done | bytes 262168
  40.5 0.7 %copy-done.7 = bf16[2,64,1024]{2,1,0:T(8,128)(2,1)} copy-done((bf16[2,64,1024]{2,1,0:T(8,128)(2,1)}, bf16[2,64,1024]{2,1,0:T(8,128)(2,1)S(1)}, u32[]{:S(2)}) %copy-start.7) | copy-done | bytes 262168
  41.7 7.8 %collective-permute-done.3.refs_3_ = bf16[2,64,1024]{2,1,0:T(8,128)(2,1)} collective-permute-done((bf16[2,64,1024]{2,1,0:T(8,128)(2,1)S(1)}, bf16[2,64,1024]{2,1,0:T(8,128)(2,1)}, u32[]{:S(2)}, u32[]{:S(2)}) %collective-permute-start.3) | collective-permute-done | bytes 262176 | tf_op jit(solution)/shard_map/ppermute | solution.py:302
  49.5 2.4 %collective-permute-start.5 = (bf16[2,64,1024]{2,1,0:T(8,128)(2,1)}, bf16[2,64,1024]{2,1,0:T(8,128)(2,1)}, u32[]{:S(2)}, u32[]{:S(2)}) collective-permute-start(bf16[2,64,1024]{2,1,0:T(8,128)(2,1)} %collective-permute-done.3.refs_3_), channel_id=1, source_target_pairs={{0,1},{1,0},{2,3},{3,2},{4,5},{5,4},{6,7},{7,6},{8,9},{9,8},{10,11... | collective-permute-start | bytes 786440 | tf_op jit(solution)/shard_map/ppermute | solution.py:259
  52.0 0.9 %copy-done.4 = bf16[2,64,1024]{2,1,0:T(8,128)(2,1)S(1)} copy-done((bf16[2,64,1024]{2,1,0:T(8,128)(2,1)S(1)}, bf16[2,64,1024]{2,1,0:T(8,128)(2,1)}, u32[]{:S(2)}) %copy-start.4) | copy-done | bytes 262168
  52.9 3.3 %shard_map.37 = (f32[8,256]{1,0:T(8,128)S(1)}, f32[8,256]{1,0:T(8,128)S(1)}, f32[1024,256]{1,0:T(8,128)S(1)}) custom-call(s32[3]{0:T(128)S(1)} %pad_add_fusion.refs_0_, bf16[256,1024]{1,0:T(8,128)(2,1)S(1)} %copy-done, bf16[256,1024]{1,0:T(8,128)(2,1)S(1)} %copy-done.1, bf16[256,1024]{1,0:T(8,128)(2,1)S(1)} %copy-done.2, bf16[2,64,1024]{2,1,0:T(8,128)(2,1)S(1)} %copy-done.4, ...), custom_call_target="tpu_custom_call" | custom-call | flops 704643072 | bytes 2883596 | tf_op jit(solution)/shard_map/pallas_call | solution.py:216
  56.2 2.1 %shard_map.38 = (f32[8,256]{1,0:T(8,128)S(1)}, f32[8,256]{1,0:T(8,128)S(1)}, f32[1024,256]{1,0:T(8,128)S(1)}) custom-call(s32[3]{0:T(128)S(1)} %pad_add_fusion.refs_0_, bf16[256,1024]{1,0:T(8,128)(2,1)S(1)} %copy-done, bf16[2,64,1024]{2,1,0:T(8,128)(2,1)S(1)} %collective-permute-done.7.next_ref.refs_2_, bf16[2,64,1024]{2,1,0:T(8,128)(2,1)S(1)} %copy-done.8, ...), custom_call_target="tpu_custom_call" | custom-call | flops 335544320 | bytes 2637836 | tf_op jit(solution)/shard_map/pallas_call | solution.py:216
  58.4 3.9 %shard_map.39 = (f32[8,256]{1,0:T(8,128)}, f32[8,256]{1,0:T(8,128)S(1)}, f32[1024,256]{1,0:T(8,128)S(1)}, bf16[2048,256]{1,0:T(8,128)(2,1)S(1)}) custom-call(s32[3]{0:T(128)S(1)} %pad_add_fusion.refs_0_, bf16[256,1024]{1,0:T(8,128)(2,1)S(1)} %copy-done, bf16[2,64,1024]{2,1,0:T(8,128)(2,1)} %collective-permute-done.1.refs_2_, ...), custom_call_target="tpu_custom_call" | custom-call | flops 603979776 | bytes 3686412 | tf_op jit(solution)/shard_map/pallas_call | solution.py:216
  62.3 2.3 %finish.1 = bf16[256,1024]{1,0:T(8,128)(2,1)} custom-call(bf16[256,1024]{1,0:T(8,128)(2,1)} %collective-permute-done.value_ref, bf16[2048,256]{1,0:T(8,128)(2,1)S(1)} %get-tuple-element.24.expo_ref, f32[8,256]{1,0:T(8,128)S(1)} %get-tuple-element.25.sum_ref, f32[1024,256]{1,0:T(8,128)S(1)} %get-tuple-element.26.acc_ref), custom_call_target="tpu_custom_call" | custom-call | flops 134217728 | bytes 2621440 | tf_op jit(solution)/shard_map/finish/pallas_call | solution.py:245
  (37 shorter events, 1.1 us)
Async XLA Ops:
  0.0 6.9 %copy-start.1 = (bf16[256,1024]{1,0:T(8,128)(2,1)S(1)}, bf16[256,1024]{1,0:T(8,128)(2,1)}, u32[]{:S(2)}) copy-start(bf16[256,1024]{1,0:T(8,128)(2,1)} %refs_2_.1) | copy-start | bytes 1572868
  0.0 7.8 %copy-start.2 = (bf16[256,1024]{1,0:T(8,128)(2,1)S(1)}, bf16[256,1024]{1,0:T(8,128)(2,1)}, u32[]{:S(2)}) copy-start(bf16[256,1024]{1,0:T(8,128)(2,1)} %refs_3_.1) | copy-start | bytes 1572868
  2.6 15.5 %collective-permute-start.2 = (bf16[2,64,1024]{2,1,0:T(8,128)(2,1)}, bf16[2,64,1024]{2,1,0:T(8,128)(2,1)S(1)}, u32[]{:S(2)}, u32[]{:S(2)}) collective-permute-start(bf16[2,64,1024]{2,1,0:T(8,128)(2,1)} %get-tuple-element.16.refs_4_), channel_id=1, source_target_pairs={{0,6},{1,7},{2,4},{3,5},{4,2},{5,3},{6,0},{7,1},{8,14},{9,15},{10,... | collective-permute-start | bytes 786440 | tf_op jit(solution)/shard_map/ppermute | solution.py:259
  6.9 13.0 %collective-permute-start.7 = (bf16[2,64,1024]{2,1,0:T(8,128)(2,1)}, bf16[2,64,1024]{2,1,0:T(8,128)(2,1)S(1)}, u32[]{:S(2)}, u32[]{:S(2)}) collective-permute-start(bf16[2,64,1024]{2,1,0:T(8,128)(2,1)} %get-tuple-element.16.refs_4_), channel_id=1, source_target_pairs={{0,2},{1,3},{2,0},{3,1},{4,6},{5,7},{6,4},{7,5},{8,10},{9,11},{10,... | collective-permute-start | bytes 786440 | tf_op jit(solution)/shard_map/ppermute | solution.py:259
  6.9 26.7 %collective-permute-start.14 = (bf16[256,1024]{1,0:T(8,128)(2,1)S(1)}, bf16[256,1024]{1,0:T(8,128)(2,1)S(1)}, u32[]{:S(2)}, u32[]{:S(2)}) collective-permute-start(bf16[256,1024]{1,0:T(8,128)(2,1)S(1)} %copy-done.1), channel_id=1, source_target_pairs={{0,1},{1,0},{2,3},{3,2},{4,5},{5,4},{6,7},{7,6},{8,9},{9,8},{10,11... | collective-permute-start | bytes 1572872 | tf_op jit(solution)/shard_map/ppermute | solution.py:259
  7.8 27.0 %collective-permute-start.15 = (bf16[256,1024]{1,0:T(8,128)(2,1)S(1)}, bf16[256,1024]{1,0:T(8,128)(2,1)S(1)}, u32[]{:S(2)}, u32[]{:S(2)}) collective-permute-start(bf16[256,1024]{1,0:T(8,128)(2,1)S(1)} %copy-done.2), channel_id=1, source_target_pairs={{0,1},{1,0},{2,3},{3,2},{4,5},{5,4},{6,7},{7,6},{8,9},{9,8},{10,11... | collective-permute-start | bytes 1572872 | tf_op jit(solution)/shard_map/ppermute | solution.py:259
  7.9 14.6 %copy-start.3 = (bf16[2,64,1024]{2,1,0:T(8,128)(2,1)S(1)}, bf16[2,64,1024]{2,1,0:T(8,128)(2,1)}, u32[]{:S(2)}) copy-start(bf16[2,64,1024]{2,1,0:T(8,128)(2,1)} %get-tuple-element.16.refs_4_) | copy-start | bytes 786436
  7.9 10.2 %collective-permute-start.6 = (bf16[2,4,1024]{2,1,0:T(4,128)(2,1)}, bf16[2,4,1024]{2,1,0:T(4,128)(2,1)S(1)}, u32[]{:S(2)}, u32[]{:S(2)}) collective-permute-start(bf16[2,4,1024]{2,1,0:T(4,128)(2,1)} %get-tuple-element.17.three_ref), channel_id=1, source_target_pairs={{0,4},{1,5},{2,6},{3,7},{4,0},{5,1},{6,2},{7,3},{8,12},{9,13},{10,... | collective-permute-start | bytes 49160 | tf_op jit(solution)/shard_map/ppermute | solution.py:259
  21.3 30.7 %copy-start = (bf16[256,1024]{1,0:T(8,128)(2,1)S(1)}, bf16[256,1024]{1,0:T(8,128)(2,1)}, u32[]{:S(2)}) copy-start(bf16[256,1024]{1,0:T(8,128)(2,1)} %refs_1_.5) | copy-start | bytes 1572868
  21.3 4.9 %collective-permute-start.8 = (bf16[2,16,1024]{2,1,0:T(8,128)(2,1)S(1)}, bf16[2,16,1024]{2,1,0:T(8,128)(2,1)S(1)}, u32[]{:S(2)}, u32[]{:S(2)}) collective-permute-start(bf16[2,16,1024]{2,1,0:T(8,128)(2,1)S(1)} %lift.1), channel_id=1, source_target_pairs={{0,8},{8,0},{16,24},{24,16},{1,9},{9,1},{17,25},{25,17},{2,10},{10... | collective-permute-start | bytes 196616 | tf_op jit(solution)/shard_map/ppermute | solution.py:259
  22.5 8.2 %collective-permute-start.1 = (bf16[2,64,1024]{2,1,0:T(8,128)(2,1)S(1)}, bf16[2,64,1024]{2,1,0:T(8,128)(2,1)}, u32[]{:S(2)}, u32[]{:S(2)}) collective-permute-start(bf16[2,64,1024]{2,1,0:T(8,128)(2,1)S(1)} %copy-done.3), channel_id=1, source_target_pairs={{0,4},{1,5},{6,2},{7,3},{8,12},{9,13},{14,10},{15,11},{16,20},{17,... | collective-permute-start | bytes 786440 | tf_op jit(solution)/shard_map/ppermute | solution.py:296
  26.2 6.2 %collective-permute-start.9 = (bf16[2,32,1024]{2,1,0:T(8,128)(2,1)S(1)}, bf16[2,32,1024]{2,1,0:T(8,128)(2,1)S(1)}, u32[]{:S(2)}, u32[]{:S(2)}) collective-permute-start(bf16[2,32,1024]{2,1,0:T(8,128)(2,1)S(1)} %pad_maximum_fusion.1), channel_id=1, source_target_pairs={{0,16},{8,24},{16,0},{24,8},{1,17},{9,25},{17,1},{25,9},{2,18},{10... | collective-permute-start | bytes 393224 | tf_op jit(solution)/shard_map/ppermute | solution.py:259
  27.5 30.9 %collective-permute-start.11 = (bf16[256,1024]{1,0:T(8,128)(2,1)S(1)}, bf16[256,1024]{1,0:T(8,128)(2,1)}, u32[]{:S(2)}, u32[]{:S(2)}) collective-permute-start(bf16[256,1024]{1,0:T(8,128)(2,1)S(1)} %copy-done.1), channel_id=1, source_target_pairs={{1,2},{3,4},{5,6},{7,8},{9,10},{11,12},{13,14},{15,16},{17,18},{19... | collective-permute-start | bytes 1572872 | tf_op jit(solution)/shard_map/ppermute | solution.py:297
  30.7 9.0 %collective-permute-start.13 = (bf16[2,64,1024]{2,1,0:T(8,128)(2,1)S(1)}, bf16[2,64,1024]{2,1,0:T(8,128)(2,1)S(1)}, u32[]{:S(2)}, u32[]{:S(2)}) collective-permute-start(bf16[2,64,1024]{2,1,0:T(8,128)(2,1)S(1)} %collective-permute-done.2.far_ref.refs_4_), channel_id=1, source_target_pairs={{0,1},{1,0},{2,3},{3,2},{4,5},{5,4},{6,7},{7,6},{8,9},{9,8},{10,11... | collective-permute-start | bytes 786440 | tf_op jit(solution)/shard_map/ppermute | solution.py:259
  32.3 8.1 %collective-permute-start.12 = (bf16[2,64,1024]{2,1,0:T(8,128)(2,1)S(1)}, bf16[2,64,1024]{2,1,0:T(8,128)(2,1)S(1)}, u32[]{:S(2)}, u32[]{:S(2)}) collective-permute-start(bf16[2,64,1024]{2,1,0:T(8,128)(2,1)S(1)} %collective-permute-done.7.next_ref.refs_2_), channel_id=1, source_target_pairs={{0,1},{1,0},{2,3},{3,2},{4,5},{5,4},{6,7},{7,6},{8,9},{9,8},{10,11... | collective-permute-start | bytes 786440 | tf_op jit(solution)/shard_map/ppermute | solution.py:259
  33.5 15.9 %collective-permute-start.3 = (bf16[2,64,1024]{2,1,0:T(8,128)(2,1)S(1)}, bf16[2,64,1024]{2,1,0:T(8,128)(2,1)}, u32[]{:S(2)}, u32[]{:S(2)}) collective-permute-start(bf16[2,64,1024]{2,1,0:T(8,128)(2,1)S(1)} %collective-permute-done.2.far_ref.refs_4_), channel_id=1, source_target_pairs={{2,0},{3,1},{4,6},{5,7},{10,8},{11,9},{12,14},{13,15},{18,16},{19,... | collective-permute-start | bytes 786440 | tf_op jit(solution)/shard_map/ppermute | solution.py:302
  34.8 27.4 %collective-permute-start = (bf16[256,1024]{1,0:T(8,128)(2,1)S(1)}, bf16[256,1024]{1,0:T(8,128)(2,1)}, u32[]{:S(2)}, u32[]{:S(2)}) collective-permute-start(bf16[256,1024]{1,0:T(8,128)(2,1)S(1)} %copy-done.2), channel_id=1, source_target_pairs={{1,2},{3,4},{5,6},{7,8},{9,10},{11,12},{13,14},{15,16},{17,18},{19... | collective-permute-start | bytes 1572872 | tf_op jit(solution)/shard_map/ppermute | solution.py:298
  40.4 17.9 %collective-permute-start.4 = (bf16[2,64,1024]{2,1,0:T(8,128)(2,1)}, bf16[2,64,1024]{2,1,0:T(8,128)(2,1)}, u32[]{:S(2)}, u32[]{:S(2)}) collective-permute-start(bf16[2,64,1024]{2,1,0:T(8,128)(2,1)} %collective-permute-done.1.refs_2_), channel_id=1, source_target_pairs={{0,1},{1,0},{2,3},{3,2},{4,5},{5,4},{6,7},{7,6},{8,9},{9,8},{10,11... | collective-permute-start | bytes 786440 | tf_op jit(solution)/shard_map/ppermute | solution.py:259
  40.5 0.7 %copy-start.7 = (bf16[2,64,1024]{2,1,0:T(8,128)(2,1)}, bf16[2,64,1024]{2,1,0:T(8,128)(2,1)S(1)}, u32[]{:S(2)}) copy-start(bf16[2,64,1024]{2,1,0:T(8,128)(2,1)S(1)} %collective-permute-done.12.refs_3_) | copy-start | bytes 786436
  41.2 17.2 %collective-permute-start.10 = (bf16[2,64,1024]{2,1,0:T(8,128)(2,1)S(1)}, bf16[2,64,1024]{2,1,0:T(8,128)(2,1)}, u32[]{:S(2)}, u32[]{:S(2)}) collective-permute-start(bf16[2,64,1024]{2,1,0:T(8,128)(2,1)S(1)} %pad_maximum_fusion.refs_6_), channel_id=1, source_target_pairs={{0,1},{1,0},{2,3},{3,2},{4,5},{5,4},{6,7},{7,6},{8,9},{9,8},{10,11... | collective-permute-start | bytes 786440 | tf_op jit(solution)/shard_map/ppermute | solution.py:259
  49.5 8.9 %collective-permute-start.5 = (bf16[2,64,1024]{2,1,0:T(8,128)(2,1)}, bf16[2,64,1024]{2,1,0:T(8,128)(2,1)}, u32[]{:S(2)}, u32[]{:S(2)}) collective-permute-start(bf16[2,64,1024]{2,1,0:T(8,128)(2,1)} %collective-permute-done.3.refs_3_), channel_id=1, source_target_pairs={{0,1},{1,0},{2,3},{3,2},{4,5},{5,4},{6,7},{7,6},{8,9},{9,8},{10,11... | collective-permute-start | bytes 786440 | tf_op jit(solution)/shard_map/ppermute | solution.py:259
  52.0 1.0 %copy-start.4 = (bf16[2,64,1024]{2,1,0:T(8,128)(2,1)S(1)}, bf16[2,64,1024]{2,1,0:T(8,128)(2,1)}, u32[]{:S(2)}) copy-start(bf16[2,64,1024]{2,1,0:T(8,128)(2,1)} %get-tuple-element.16.refs_4_) | copy-start | bytes 786436
  52.9 3.3 %copy-start.6 = (bf16[2,64,1024]{2,1,0:T(8,128)(2,1)S(1)}, bf16[2,64,1024]{2,1,0:T(8,128)(2,1)}, u32[]{:S(2)}) copy-start(bf16[2,64,1024]{2,1,0:T(8,128)(2,1)} %copy-done.5) | copy-start | bytes 786436
  52.9 3.3 %copy-start.8 = (bf16[2,64,1024]{2,1,0:T(8,128)(2,1)S(1)}, bf16[2,64,1024]{2,1,0:T(8,128)(2,1)}, u32[]{:S(2)}) copy-start(bf16[2,64,1024]{2,1,0:T(8,128)(2,1)} %copy-done.7) | copy-start | bytes 786436
  (2 other events, 1.4 us)
where the time goes:
time: 64.9 us; the launch traced here: 64.6 us
  starting transfers between devices  26.9 us (41%)
  waiting for transfers between devices  19.5 us (30%)
  Pallas kernels  14.9 us (23%)
  local copies, waits for them, and re-layouts  3.11 us (5%)
    ppermute x12, starting transfers between devices, swap(): lax.ppermute(x, axis, [(i, i ^ mask) for i in range(lax.axis_size(axis))])  13.9 us
    ppermute x12, waiting for transfers between devices, swap(): lax.ppermute(x, axis, [(i, i ^ mask) for i in range(lax.axis_size(axis))])  11.7 us
    pallas_call x3, Pallas kernels, stage(): pl.pallas_call(functools.partial(stage_kernel, plan, state is None), out_...  9.26 us
    ppermute x1, waiting for transfers between devices, attend(): lax.ppermute(one_far, 'seqb', [(i, i ^ 2) for i, chip in chips if chip in...  7.78 us
    ppermute x1, starting transfers between devices, attend(): across_values = lax.ppermute(value_rows, AXES, bounds)  4.84 us
    ppermute x1, starting transfers between devices, attend(): lax.ppermute(own_one, 'seqb', [(i, i ^ 4) for i, chip in chips if chip in...  3.62 us
    ppermute x1, starting transfers between devices, attend(): across_keys = lax.ppermute(key_rows, AXES, bounds)  3.21 us
    unnamed x20, local copies, waits for them, and re-layouts  3.11 us
  transfers between devices with their start and end apart: 16, of which 3 were waited for; matrix products, arithmetic and copies ran while one was open for 0% of the time, Pallas kernels for 15%

commit v1 on v0

--- a/solution.py
+++ b/solution.py
@@ -17,7 +17,9 @@
 NEG = -1e30
 EXP2_SCALE = 1.4426950408889634 / HEAD_DIM**0.5
 VMEM_LIMIT = 24 << 20
-POOL_LIMIT = 67043328 - (7 << 18)
+POOL_LIMIT = 24 << 20
+POOL_PARTS = 1
+OUT_PARTS = 2
 
 
 def pool_rows(rows):
@@ -29,17 +31,21 @@
 
 
 def pool_kernel(k_ref, v_ref, one_ref, three_ref, rows_ref, sem):
-    copies = [
-        pltpu.make_async_copy(rows, rows_ref.at[side], sem.at[side])
-        for side, rows in enumerate((k_ref, v_ref))
-    ]
-    for copy in copies:
-        copy.start()
-    for side, copy in enumerate(copies):
+    part = rows_ref.shape[1] // POOL_PARTS
+    copies = {}
+    for at in range(POOL_PARTS):
+        for side, ref in enumerate((k_ref, v_ref)):
+            rows = pl.ds(at * part, part)
+            copies[at, side] = pltpu.make_async_copy(
+                ref.at[rows, :], rows_ref.at[side, rows, :], sem.at[at, side]
+            )
+            copies[at, side].start()
+    for (at, side), copy in copies.items():
         copy.wait()
-        one = pool_rows(rows_ref[side])
-        one_ref[side] = one
-        three_ref[side] = pool_rows(pool_rows(one))
+        one = pool_rows(rows_ref[side, pl.ds(at * part, part), :])
+        one_ref[side, pl.ds(at * part // POOL, part // POOL), :] = one
+    for side in range(2):
+        three_ref[side] = pool_rows(pool_rows(one_ref[side]))
 
 
 def pool_call(key_rows, value_rows):
@@ -52,7 +58,7 @@
         out_shape=[jax.ShapeDtypeStruct(shape, jnp.bfloat16) for shape in shapes],
         scratch_shapes=[
             pltpu.VMEM((2, rows, width), jnp.bfloat16),
-            pltpu.SemaphoreType.DMA((2,)),
+            pltpu.SemaphoreType.DMA((POOL_PARTS, 2)),
         ],
         name="pool_own",
         compiler_params=pltpu.CompilerParams(vmem_limit_bytes=POOL_LIMIT),
@@ -231,13 +237,24 @@
     )(*operands)
 
 
-def finish_kernel(value_ref, expo_ref, sum_ref, acc_ref, out_ref):
-    tok = out_ref.shape[0]
+def finish_kernel(value_ref, expo_ref, sum_ref, acc_ref, out_ref, rows_ref, sem):
+    tok = rows_ref.shape[0]
+    width = rows_ref.shape[1] // OUT_PARTS
+    copies = []
     for head in range(HEADS):
         cols = pl.ds(head * HEAD_DIM, HEAD_DIM)
         mixed = weighted(value_ref[:, cols], expo_ref[pl.ds(head * tok, tok), :]) + acc_ref[cols, :]
         mixed = mixed * (1.0 / sum_ref[pl.ds(head, 1), :])
-        out_ref[:, cols] = mixed.T.astype(jnp.bfloat16)
+        rows_ref[:, cols] = mixed.T.astype(jnp.bfloat16)
+        if (head + 1) * OUT_PARTS % HEADS == 0:
+            part = (head + 1) * OUT_PARTS // HEADS - 1
+            done = pl.ds(part * width, width)
+            copies.append(
+                pltpu.make_async_copy(rows_ref.at[:, done], out_ref.at[:, done], sem.at[part])
+            )
+            copies[-1].start()
+    for copy in copies:
+        copy.wait()
 
 
 def finish(values, expo, total, mixed):
@@ -246,7 +263,11 @@
         finish_kernel,
         out_shape=jax.ShapeDtypeStruct((tok, width), jnp.bfloat16),
         in_specs=[pl.BlockSpec(memory_space=pltpu.VMEM)] * 4,
-        out_specs=pl.BlockSpec(memory_space=pltpu.VMEM),
+        out_specs=pl.BlockSpec(memory_space=pltpu.HBM),
+        scratch_shapes=[
+            pltpu.VMEM((tok, width), jnp.bfloat16),
+            pltpu.SemaphoreType.DMA((OUT_PARTS,)),
+        ],
         name="finish",
         compiler_params=pltpu.CompilerParams(vmem_limit_bytes=VMEM_LIMIT),
         cost_estimate=pl.CostEstimate(

time: 64.9 us -> 62.8 us (0.968)
  Pallas kernels: 14.9 us -> 13.5 us
  local copies, waits for them, and re-layouts: 3.11 us -> 2.38 us
    pallas_call x1, Pallas kernels: 2.32 us -> 1.23 us  [finish(): pl.pallas_call(finish_kernel, out_shape=jax.ShapeDtypeStruct((tok, width)...]
    pallas_call x1, Pallas kernels: 2.64 us -> 1.76 us  [pool_call(): pl.pallas_call(pool_kernel, in_specs=[pl.BlockSpec(memory_space=pltpu.HBM...]
    unnamed x20 -> x14, local copies, waits for them, and re-layouts: 3.11 us -> 2.38 us
  transfers between devices with their start and end apart: 16 -> 16, of which waited for: 3 -> 3; matrix products, arithmetic and copies ran while one was open for 0% -> 0% of each run, Pallas kernels for 15% -> 17%
where the time goes in v1:
time: 62.8 us; the launch traced here: 62.5 us
  starting transfers between devices  27 us (43%)
  waiting for transfers between devices  19.4 us (31%)
  Pallas kernels  13.5 us (21%)
  local copies, waits for them, and re-layouts  2.38 us (4%)
    ppermute x12, starting transfers between devices, swap(): lax.ppermute(x, axis, [(i, i ^ mask) for i in range(lax.axis_size(axis))])  14.1 us
    ppermute x12, waiting for transfers between devices, swap(): lax.ppermute(x, axis, [(i, i ^ mask) for i in range(lax.axis_size(axis))])  11.5 us
    pallas_call x3, Pallas kernels, stage(): pl.pallas_call(functools.partial(stage_kernel, plan, state is None), out_...  9.83 us
    ppermute x1, waiting for transfers between devices, attend(): lax.ppermute(one_far, 'seqb', [(i, i ^ 2) for i, chip in chips if chip in...  7.81 us
    ppermute x1, starting transfers between devices, attend(): across_values = lax.ppermute(value_rows, AXES, bounds)  4.83 us
    ppermute x1, starting transfers between devices, attend(): lax.ppermute(own_one, 'seqb', [(i, i ^ 4) for i, chip in chips if chip in...  3.63 us
    ppermute x1, starting transfers between devices, attend(): across_keys = lax.ppermute(key_rows, AXES, bounds)  3.21 us
    unnamed x14, local copies, waits for them, and re-layouts  2.38 us
  transfers between devices with their start and end apart: 16, of which 3 were waited for; matrix products, arithmetic and copies ran while one was open for 0% of the time, Pallas kernels for 17%

profile of v1, /device:TPU:1, one launch (start us, length us, event | category | flops | bytes accessed | tf_op | source)
XLA Modules:
  0.0 62.5 jit_solution(15210895972505953139)
XLA Ops:
  0.0 1.8 %pool_own.1 = (bf16[2,64,1024]{2,1,0:T(8,128)(2,1)S(1)}, bf16[2,4,1024]{2,1,0:T(4,128)(2,1)S(1)}) custom-call(bf16[256,1024]{1,0:T(8,128)(2,1)} %refs_2_.1, bf16[256,1024]{1,0:T(8,128)(2,1)} %refs_3_.1), custom_call_target="tpu_custom_call" | custom-call | flops 67108864 | bytes 1310720 | tf_op jit(solution)/shard_map/pool_own/pallas_call | solution.py:54
  1.8 4.2 %collective-permute-start.2 = (bf16[2,64,1024]{2,1,0:T(8,128)(2,1)S(1)}, bf16[2,64,1024]{2,1,0:T(8,128)(2,1)S(1)}, u32[]{:S(2)}, u32[]{:S(2)}) collective-permute-start(bf16[2,64,1024]{2,1,0:T(8,128)(2,1)S(1)} %get-tuple-element.16.refs_4_), channel_id=1, source_target_pairs={{0,6},{1,7},{2,4},{3,5},{4,2},{5,3},{6,0},{7,1},{8,14},{9,15},{10,... | collective-permute-start | bytes 786440 | tf_op jit(solution)/shard_map/ppermute | solution.py:280
  6.0 1.0 %collective-permute-start.14 = (bf16[256,1024]{1,0:T(8,128)(2,1)}, bf16[256,1024]{1,0:T(8,128)(2,1)S(1)}, u32[]{:S(2)}, u32[]{:S(2)}) collective-permute-start(bf16[256,1024]{1,0:T(8,128)(2,1)} %refs_2_.1), channel_id=1, source_target_pairs={{0,1},{1,0},{2,3},{3,2},{4,5},{5,4},{6,7},{7,6},{8,9},{9,8},{10,11... | collective-permute-start | bytes 1572872 | tf_op jit(solution)/shard_map/ppermute | solution.py:280
  7.3 9.7 %collective-permute-done.6.other_ref = bf16[2,4,1024]{2,1,0:T(4,128)(2,1)S(1)} collective-permute-done((bf16[2,4,1024]{2,1,0:T(4,128)(2,1)S(1)}, bf16[2,4,1024]{2,1,0:T(4,128)(2,1)S(1)}, u32[]{:S(2)}, u32[]{:S(2)}) %collective-permute-start.6) | collective-permute-done | bytes 16416 | tf_op jit(solution)/shard_map/ppermute | solution.py:280
  17.0 1.8 %collective-permute-done.7.next_ref.refs_2_ = bf16[2,64,1024]{2,1,0:T(8,128)(2,1)S(1)} collective-permute-done((bf16[2,64,1024]{2,1,0:T(8,128)(2,1)S(1)}, bf16[2,64,1024]{2,1,0:T(8,128)(2,1)S(1)}, u32[]{:S(2)}, u32[]{:S(2)}) %collective-permute-start.7) | collective-permute-done | bytes 262176 | tf_op jit(solution)/shard_map/ppermute | solution.py:280
  18.8 0.7 %lift.1 = bf16[2,16,1024]{2,1,0:T(8,128)(2,1)S(1)} custom-call(bf16[2,4,1024]{2,1,0:T(4,128)(2,1)S(1)} %get-tuple-element.17.three_ref, bf16[2,4,1024]{2,1,0:T(4,128)(2,1)S(1)} %collective-permute-done.6.other_ref, bf16[2,64,1024]{2,1,0:T(8,128)(2,1)S(1)} %collective-permute-done.7.next_ref.refs_2_, ...), custom_call_target="tpu_custom_call" | custom-call | flops 16777216 | bytes 1228800 | tf_op jit(solution)/shard_map/lift/pallas_call | solution.py:82
  19.5 1.2 %collective-permute-start.8 = (bf16[2,16,1024]{2,1,0:T(8,128)(2,1)S(1)}, bf16[2,16,1024]{2,1,0:T(8,128)(2,1)S(1)}, u32[]{:S(2)}, u32[]{:S(2)}) collective-permute-start(bf16[2,16,1024]{2,1,0:T(8,128)(2,1)S(1)} %lift.1), channel_id=1, source_target_pairs={{0,8},{8,0},{16,24},{24,16},{1,9},{9,1},{17,25},{25,17},{2,10},{10... | collective-permute-start | bytes 196616 | tf_op jit(solution)/shard_map/ppermute | solution.py:280
  20.7 3.6 %collective-permute-start.1 = (bf16[2,64,1024]{2,1,0:T(8,128)(2,1)S(1)}, bf16[2,64,1024]{2,1,0:T(8,128)(2,1)}, u32[]{:S(2)}, u32[]{:S(2)}) collective-permute-start(bf16[2,64,1024]{2,1,0:T(8,128)(2,1)S(1)} %get-tuple-element.16.refs_4_), channel_id=1, source_target_pairs={{0,4},{1,5},{6,2},{7,3},{8,12},{9,13},{14,10},{15,11},{16,20},{17,... | collective-permute-start | bytes 786440 | tf_op jit(solution)/shard_map/ppermute | solution.py:317
  24.4 1.3 %collective-permute-start.9 = (bf16[2,32,1024]{2,1,0:T(8,128)(2,1)S(1)}, bf16[2,32,1024]{2,1,0:T(8,128)(2,1)S(1)}, u32[]{:S(2)}, u32[]{:S(2)}) collective-permute-start(bf16[2,32,1024]{2,1,0:T(8,128)(2,1)S(1)} %pad_maximum_fusion.1), channel_id=1, source_target_pairs={{0,16},{8,24},{16,0},{24,8},{1,17},{9,25},{17,1},{25,9},{2,18},{10... | collective-permute-start | bytes 393224 | tf_op jit(solution)/shard_map/ppermute | solution.py:280
  25.7 3.2 %collective-permute-start.11 = (bf16[256,1024]{1,0:T(8,128)(2,1)}, bf16[256,1024]{1,0:T(8,128)(2,1)S(1)}, u32[]{:S(2)}, u32[]{:S(2)}) collective-permute-start(bf16[256,1024]{1,0:T(8,128)(2,1)} %refs_2_.1), channel_id=1, source_target_pairs={{1,2},{3,4},{5,6},{7,8},{9,10},{11,12},{13,14},{15,16},{17,18},{19... | collective-permute-start | bytes 1572872 | tf_op jit(solution)/shard_map/ppermute | solution.py:318
  28.9 1.4 %collective-permute-start.13 = (bf16[2,64,1024]{2,1,0:T(8,128)(2,1)S(1)}, bf16[2,64,1024]{2,1,0:T(8,128)(2,1)S(1)}, u32[]{:S(2)}, u32[]{:S(2)}) collective-permute-start(bf16[2,64,1024]{2,1,0:T(8,128)(2,1)S(1)} %collective-permute-done.2.far_ref.refs_4_), channel_id=1, source_target_pairs={{0,1},{1,0},{2,3},{3,2},{4,5},{5,4},{6,7},{7,6},{8,9},{9,8},{10,11... | collective-permute-start | bytes 786440 | tf_op jit(solution)/shard_map/ppermute | solution.py:280
  30.3 1.4 %collective-permute-start.12 = (bf16[2,64,1024]{2,1,0:T(8,128)(2,1)S(1)}, bf16[2,64,1024]{2,1,0:T(8,128)(2,1)S(1)}, u32[]{:S(2)}, u32[]{:S(2)}) collective-permute-start(bf16[2,64,1024]{2,1,0:T(8,128)(2,1)S(1)} %collective-permute-done.7.next_ref.refs_2_), channel_id=1, source_target_pairs={{0,1},{1,0},{2,3},{3,2},{4,5},{5,4},{6,7},{7,6},{8,9},{9,8},{10,11... | collective-permute-start | bytes 786440 | tf_op jit(solution)/shard_map/ppermute | solution.py:280
  31.8 1.3 %collective-permute-start.3 = (bf16[2,64,1024]{2,1,0:T(8,128)(2,1)S(1)}, bf16[2,64,1024]{2,1,0:T(8,128)(2,1)}, u32[]{:S(2)}, u32[]{:S(2)}) collective-permute-start(bf16[2,64,1024]{2,1,0:T(8,128)(2,1)S(1)} %collective-permute-done.2.far_ref.refs_4_), channel_id=1, source_target_pairs={{2,0},{3,1},{4,6},{5,7},{10,8},{11,9},{12,14},{13,15},{18,16},{19,... | collective-permute-start | bytes 786440 | tf_op jit(solution)/shard_map/ppermute | solution.py:323
  33.1 4.8 %collective-permute-start = (bf16[256,1024]{1,0:T(8,128)(2,1)}, bf16[256,1024]{1,0:T(8,128)(2,1)S(1)}, u32[]{:S(2)}, u32[]{:S(2)}) collective-permute-start(bf16[256,1024]{1,0:T(8,128)(2,1)} %refs_3_.1), channel_id=1, source_target_pairs={{1,2},{3,4},{5,6},{7,8},{9,10},{11,12},{13,14},{15,16},{17,18},{19... | collective-permute-start | bytes 1572872 | tf_op jit(solution)/shard_map/ppermute | solution.py:319
  37.9 0.7 %copy-done.3 = bf16[2,64,1024]{2,1,0:T(8,128)(2,1)} copy-done((bf16[2,64,1024]{2,1,0:T(8,128)(2,1)}, bf16[2,64,1024]{2,1,0:T(8,128)(2,1)S(1)}, u32[]{:S(2)}) %copy-start.3) | copy-done | bytes 262168
  38.7 0.7 %copy-done.5 = bf16[2,64,1024]{2,1,0:T(8,128)(2,1)} copy-done((bf16[2,64,1024]{2,1,0:T(8,128)(2,1)}, bf16[2,64,1024]{2,1,0:T(8,128)(2,1)S(1)}, u32[]{:S(2)}) %copy-start.5) | copy-done | bytes 262168
  39.4 0.5 collective-permute-start.10
  39.9 7.8 %collective-permute-done.3.refs_3_ = bf16[2,64,1024]{2,1,0:T(8,128)(2,1)} collective-permute-done((bf16[2,64,1024]{2,1,0:T(8,128)(2,1)S(1)}, bf16[2,64,1024]{2,1,0:T(8,128)(2,1)}, u32[]{:S(2)}, u32[]{:S(2)}) %collective-permute-start.3) | collective-permute-done | bytes 262176 | tf_op jit(solution)/shard_map/ppermute | solution.py:323
  47.7 2.6 %collective-permute-start.5 = (bf16[2,64,1024]{2,1,0:T(8,128)(2,1)}, bf16[2,64,1024]{2,1,0:T(8,128)(2,1)}, u32[]{:S(2)}, u32[]{:S(2)}) collective-permute-start(bf16[2,64,1024]{2,1,0:T(8,128)(2,1)} %collective-permute-done.3.refs_3_), channel_id=1, source_target_pairs={{0,1},{1,0},{2,3},{3,2},{4,5},{5,4},{6,7},{7,6},{8,9},{9,8},{10,11... | collective-permute-start | bytes 786440 | tf_op jit(solution)/shard_map/ppermute | solution.py:280
  50.4 0.9 %copy-done.2 = bf16[2,64,1024]{2,1,0:T(8,128)(2,1)S(1)} copy-done((bf16[2,64,1024]{2,1,0:T(8,128)(2,1)S(1)}, bf16[2,64,1024]{2,1,0:T(8,128)(2,1)}, u32[]{:S(2)}) %copy-start.2) | copy-done | bytes 262168
  51.4 4.0 %shard_map.37 = (f32[8,256]{1,0:T(8,128)S(1)}, f32[8,256]{1,0:T(8,128)S(1)}, f32[1024,256]{1,0:T(8,128)S(1)}) custom-call(s32[3]{0:T(128)S(1)} %pad_add_fusion.refs_0_, bf16[256,1024]{1,0:T(8,128)(2,1)S(1)} %copy-done, bf16[256,1024]{1,0:T(8,128)(2,1)} %refs_2_.1, bf16[256,1024]{1,0:T(8,128)(2,1)} %refs_3_.1, bf16[2,64,1024]{2,1,0:T(8,128)(2,1)S(1)} %copy-done.2, ...), custom_call_target="tpu_custom_call" | custom-call | flops 704643072 | bytes 2883596 | tf_op jit(solution)/shard_map/pallas_call | solution.py:222
  55.4 2.1 %shard_map.38 = (f32[8,256]{1,0:T(8,128)S(1)}, f32[8,256]{1,0:T(8,128)S(1)}, f32[1024,256]{1,0:T(8,128)S(1)}) custom-call(s32[3]{0:T(128)S(1)} %pad_add_fusion.refs_0_, bf16[256,1024]{1,0:T(8,128)(2,1)S(1)} %copy-done, bf16[2,64,1024]{2,1,0:T(8,128)(2,1)S(1)} %collective-permute-done.7.next_ref.refs_2_, bf16[2,64,1024]{2,1,0:T(8,128)(2,1)S(1)} %copy-done.6, ...), custom_call_target="tpu_custom_call" | custom-call | flops 335544320 | bytes 2637836 | tf_op jit(solution)/shard_map/pallas_call | solution.py:222
  57.5 3.7 %shard_map.39 = (f32[8,256]{1,0:T(8,128)}, f32[8,256]{1,0:T(8,128)S(1)}, f32[1024,256]{1,0:T(8,128)S(1)}, bf16[2048,256]{1,0:T(8,128)(2,1)S(1)}) custom-call(s32[3]{0:T(128)S(1)} %pad_add_fusion.refs_0_, bf16[256,1024]{1,0:T(8,128)(2,1)S(1)} %copy-done, bf16[2,64,1024]{2,1,0:T(8,128)(2,1)} %collective-permute-done.1.refs_2_, ...), custom_call_target="tpu_custom_call" | custom-call | flops 603979776 | bytes 3686412 | tf_op jit(solution)/shard_map/pallas_call | solution.py:222
  61.3 1.2 %finish.1 = bf16[256,1024]{1,0:T(8,128)(2,1)} custom-call(bf16[256,1024]{1,0:T(8,128)(2,1)S(1)} %collective-permute-done.value_ref, bf16[2048,256]{1,0:T(8,128)(2,1)S(1)} %get-tuple-element.24.expo_ref, f32[8,256]{1,0:T(8,128)S(1)} %get-tuple-element.25.sum_ref, f32[1024,256]{1,0:T(8,128)S(1)} %get-tuple-element.26.acc_ref), custom_call_target="tpu_custom_call" | custom-call | flops 134217728 | bytes 2621440 | tf_op jit(solution)/shard_map/finish/pallas_call | solution.py:262
  (31 shorter events, 0.5 us)
Async XLA Ops:
  1.8 19.0 %copy-start.1 = (bf16[2,64,1024]{2,1,0:T(8,128)(2,1)}, bf16[2,64,1024]{2,1,0:T(8,128)(2,1)S(1)}, u32[]{:S(2)}) copy-start(bf16[2,64,1024]{2,1,0:T(8,128)(2,1)S(1)} %get-tuple-element.16.refs_4_) | copy-start | bytes 786436
  1.8 15.3 %collective-permute-start.2 = (bf16[2,64,1024]{2,1,0:T(8,128)(2,1)S(1)}, bf16[2,64,1024]{2,1,0:T(8,128)(2,1)S(1)}, u32[]{:S(2)}, u32[]{:S(2)}) collective-permute-start(bf16[2,64,1024]{2,1,0:T(8,128)(2,1)S(1)} %get-tuple-element.16.refs_4_), channel_id=1, source_target_pairs={{0,6},{1,7},{2,4},{3,5},{4,2},{5,3},{6,0},{7,1},{8,14},{9,15},{10,... | collective-permute-start | bytes 786440 | tf_op jit(solution)/shard_map/ppermute | solution.py:280
  6.0 12.8 %collective-permute-start.7 = (bf16[2,64,1024]{2,1,0:T(8,128)(2,1)S(1)}, bf16[2,64,1024]{2,1,0:T(8,128)(2,1)S(1)}, u32[]{:S(2)}, u32[]{:S(2)}) collective-permute-start(bf16[2,64,1024]{2,1,0:T(8,128)(2,1)S(1)} %get-tuple-element.16.refs_4_), channel_id=1, source_target_pairs={{0,2},{1,3},{2,0},{3,1},{4,6},{5,7},{6,4},{7,5},{8,10},{9,11},{10,... | collective-permute-start | bytes 786440 | tf_op jit(solution)/shard_map/ppermute | solution.py:280
  6.0 25.8 %collective-permute-start.14 = (bf16[256,1024]{1,0:T(8,128)(2,1)}, bf16[256,1024]{1,0:T(8,128)(2,1)S(1)}, u32[]{:S(2)}, u32[]{:S(2)}) collective-permute-start(bf16[256,1024]{1,0:T(8,128)(2,1)} %refs_2_.1), channel_id=1, source_target_pairs={{0,1},{1,0},{2,3},{3,2},{4,5},{5,4},{6,7},{7,6},{8,9},{9,8},{10,11... | collective-permute-start | bytes 1572872 | tf_op jit(solution)/shard_map/ppermute | solution.py:280
  6.9 26.1 %collective-permute-start.15 = (bf16[256,1024]{1,0:T(8,128)(2,1)}, bf16[256,1024]{1,0:T(8,128)(2,1)S(1)}, u32[]{:S(2)}, u32[]{:S(2)}) collective-permute-start(bf16[256,1024]{1,0:T(8,128)(2,1)} %refs_3_.1), channel_id=1, source_target_pairs={{0,1},{1,0},{2,3},{3,2},{4,5},{5,4},{6,7},{7,6},{8,9},{9,8},{10,11... | collective-permute-start | bytes 1572872 | tf_op jit(solution)/shard_map/ppermute | solution.py:280
  6.9 10.1 %collective-permute-start.6 = (bf16[2,4,1024]{2,1,0:T(4,128)(2,1)S(1)}, bf16[2,4,1024]{2,1,0:T(4,128)(2,1)S(1)}, u32[]{:S(2)}, u32[]{:S(2)}) collective-permute-start(bf16[2,4,1024]{2,1,0:T(4,128)(2,1)S(1)} %get-tuple-element.17.three_ref), channel_id=1, source_target_pairs={{0,4},{1,5},{2,6},{3,7},{4,0},{5,1},{6,2},{7,3},{8,12},{9,13},{10,... | collective-permute-start | bytes 49160 | tf_op jit(solution)/shard_map/ppermute | solution.py:280
  19.5 30.9 %copy-start = (bf16[256,1024]{1,0:T(8,128)(2,1)S(1)}, bf16[256,1024]{1,0:T(8,128)(2,1)}, u32[]{:S(2)}) copy-start(bf16[256,1024]{1,0:T(8,128)(2,1)} %refs_1_.5) | copy-start | bytes 1572868
  19.5 4.9 %collective-permute-start.8 = (bf16[2,16,1024]{2,1,0:T(8,128)(2,1)S(1)}, bf16[2,16,1024]{2,1,0:T(8,128)(2,1)S(1)}, u32[]{:S(2)}, u32[]{:S(2)}) collective-permute-start(bf16[2,16,1024]{2,1,0:T(8,128)(2,1)S(1)} %lift.1), channel_id=1, source_target_pairs={{0,8},{8,0},{16,24},{24,16},{1,9},{9,1},{17,25},{25,17},{2,10},{10... | collective-permute-start | bytes 196616 | tf_op jit(solution)/shard_map/ppermute | solution.py:280
  20.7 8.2 %collective-permute-start.1 = (bf16[2,64,1024]{2,1,0:T(8,128)(2,1)S(1)}, bf16[2,64,1024]{2,1,0:T(8,128)(2,1)}, u32[]{:S(2)}, u32[]{:S(2)}) collective-permute-start(bf16[2,64,1024]{2,1,0:T(8,128)(2,1)S(1)} %get-tuple-element.16.refs_4_), channel_id=1, source_target_pairs={{0,4},{1,5},{6,2},{7,3},{8,12},{9,13},{14,10},{15,11},{16,20},{17,... | collective-permute-start | bytes 786440 | tf_op jit(solution)/shard_map/ppermute | solution.py:317
  24.4 6.0 %collective-permute-start.9 = (bf16[2,32,1024]{2,1,0:T(8,128)(2,1)S(1)}, bf16[2,32,1024]{2,1,0:T(8,128)(2,1)S(1)}, u32[]{:S(2)}, u32[]{:S(2)}) collective-permute-start(bf16[2,32,1024]{2,1,0:T(8,128)(2,1)S(1)} %pad_maximum_fusion.1), channel_id=1, source_target_pairs={{0,16},{8,24},{16,0},{24,8},{1,17},{9,25},{17,1},{25,9},{2,18},{10... | collective-permute-start | bytes 393224 | tf_op jit(solution)/shard_map/ppermute | solution.py:280
  25.7 31.8 %collective-permute-start.11 = (bf16[256,1024]{1,0:T(8,128)(2,1)}, bf16[256,1024]{1,0:T(8,128)(2,1)S(1)}, u32[]{:S(2)}, u32[]{:S(2)}) collective-permute-start(bf16[256,1024]{1,0:T(8,128)(2,1)} %refs_2_.1), channel_id=1, source_target_pairs={{1,2},{3,4},{5,6},{7,8},{9,10},{11,12},{13,14},{15,16},{17,18},{19... | collective-permute-start | bytes 1572872 | tf_op jit(solution)/shard_map/ppermute | solution.py:318
  28.9 9.0 %collective-permute-start.13 = (bf16[2,64,1024]{2,1,0:T(8,128)(2,1)S(1)}, bf16[2,64,1024]{2,1,0:T(8,128)(2,1)S(1)}, u32[]{:S(2)}, u32[]{:S(2)}) collective-permute-start(bf16[2,64,1024]{2,1,0:T(8,128)(2,1)S(1)} %collective-permute-done.2.far_ref.refs_4_), channel_id=1, source_target_pairs={{0,1},{1,0},{2,3},{3,2},{4,5},{5,4},{6,7},{7,6},{8,9},{9,8},{10,11... | collective-permute-start | bytes 786440 | tf_op jit(solution)/shard_map/ppermute | solution.py:280
  30.3 8.3 %collective-permute-start.12 = (bf16[2,64,1024]{2,1,0:T(8,128)(2,1)S(1)}, bf16[2,64,1024]{2,1,0:T(8,128)(2,1)S(1)}, u32[]{:S(2)}, u32[]{:S(2)}) collective-permute-start(bf16[2,64,1024]{2,1,0:T(8,128)(2,1)S(1)} %collective-permute-done.7.next_ref.refs_2_), channel_id=1, source_target_pairs={{0,1},{1,0},{2,3},{3,2},{4,5},{5,4},{6,7},{7,6},{8,9},{9,8},{10,11... | collective-permute-start | bytes 786440 | tf_op jit(solution)/shard_map/ppermute | solution.py:280
  31.8 15.9 %collective-permute-start.3 = (bf16[2,64,1024]{2,1,0:T(8,128)(2,1)S(1)}, bf16[2,64,1024]{2,1,0:T(8,128)(2,1)}, u32[]{:S(2)}, u32[]{:S(2)}) collective-permute-start(bf16[2,64,1024]{2,1,0:T(8,128)(2,1)S(1)} %collective-permute-done.2.far_ref.refs_4_), channel_id=1, source_target_pairs={{2,0},{3,1},{4,6},{5,7},{10,8},{11,9},{12,14},{13,15},{18,16},{19,... | collective-permute-start | bytes 786440 | tf_op jit(solution)/shard_map/ppermute | solution.py:323
  33.1 28.2 %collective-permute-start = (bf16[256,1024]{1,0:T(8,128)(2,1)}, bf16[256,1024]{1,0:T(8,128)(2,1)S(1)}, u32[]{:S(2)}, u32[]{:S(2)}) collective-permute-start(bf16[256,1024]{1,0:T(8,128)(2,1)} %refs_3_.1), channel_id=1, source_target_pairs={{1,2},{3,4},{5,6},{7,8},{9,10},{11,12},{13,14},{15,16},{17,18},{19... | collective-permute-start | bytes 1572872 | tf_op jit(solution)/shard_map/ppermute | solution.py:319
  37.9 0.7 %copy-start.3 = (bf16[2,64,1024]{2,1,0:T(8,128)(2,1)}, bf16[2,64,1024]{2,1,0:T(8,128)(2,1)S(1)}, u32[]{:S(2)}) copy-start(bf16[2,64,1024]{2,1,0:T(8,128)(2,1)S(1)} %collective-permute-done.13.refs_5_) | copy-start | bytes 786436
  38.7 18.8 %collective-permute-start.4 = (bf16[2,64,1024]{2,1,0:T(8,128)(2,1)}, bf16[2,64,1024]{2,1,0:T(8,128)(2,1)}, u32[]{:S(2)}, u32[]{:S(2)}) collective-permute-start(bf16[2,64,1024]{2,1,0:T(8,128)(2,1)} %collective-permute-done.1.refs_2_), channel_id=1, source_target_pairs={{0,1},{1,0},{2,3},{3,2},{4,5},{5,4},{6,7},{7,6},{8,9},{9,8},{10,11... | collective-permute-start | bytes 786440 | tf_op jit(solution)/shard_map/ppermute | solution.py:280
  38.7 0.7 %copy-start.5 = (bf16[2,64,1024]{2,1,0:T(8,128)(2,1)}, bf16[2,64,1024]{2,1,0:T(8,128)(2,1)S(1)}, u32[]{:S(2)}) copy-start(bf16[2,64,1024]{2,1,0:T(8,128)(2,1)S(1)} %collective-permute-done.12.refs_3_) | copy-start | bytes 786436
  39.4 18.1 %collective-permute-start.10 = (bf16[2,64,1024]{2,1,0:T(8,128)(2,1)S(1)}, bf16[2,64,1024]{2,1,0:T(8,128)(2,1)}, u32[]{:S(2)}, u32[]{:S(2)}) collective-permute-start(bf16[2,64,1024]{2,1,0:T(8,128)(2,1)S(1)} %pad_maximum_fusion.refs_6_), channel_id=1, source_target_pairs={{0,1},{1,0},{2,3},{3,2},{4,5},{5,4},{6,7},{7,6},{8,9},{9,8},{10,11... | collective-permute-start | bytes 786440 | tf_op jit(solution)/shard_map/ppermute | solution.py:280
  47.7 9.8 %collective-permute-start.5 = (bf16[2,64,1024]{2,1,0:T(8,128)(2,1)}, bf16[2,64,1024]{2,1,0:T(8,128)(2,1)}, u32[]{:S(2)}, u32[]{:S(2)}) collective-permute-start(bf16[2,64,1024]{2,1,0:T(8,128)(2,1)} %collective-permute-done.3.refs_3_), channel_id=1, source_target_pairs={{0,1},{1,0},{2,3},{3,2},{4,5},{5,4},{6,7},{7,6},{8,9},{9,8},{10,11... | collective-permute-start | bytes 786440 | tf_op jit(solution)/shard_map/ppermute | solution.py:280
  50.4 1.0 %copy-start.2 = (bf16[2,64,1024]{2,1,0:T(8,128)(2,1)S(1)}, bf16[2,64,1024]{2,1,0:T(8,128)(2,1)}, u32[]{:S(2)}) copy-start(bf16[2,64,1024]{2,1,0:T(8,128)(2,1)} %copy-done.1) | copy-start | bytes 786436
  51.3 4.0 %copy-start.4 = (bf16[2,64,1024]{2,1,0:T(8,128)(2,1)S(1)}, bf16[2,64,1024]{2,1,0:T(8,128)(2,1)}, u32[]{:S(2)}) copy-start(bf16[2,64,1024]{2,1,0:T(8,128)(2,1)} %copy-done.3) | copy-start | bytes 786436
  51.4 4.0 %copy-start.6 = (bf16[2,64,1024]{2,1,0:T(8,128)(2,1)S(1)}, bf16[2,64,1024]{2,1,0:T(8,128)(2,1)}, u32[]{:S(2)}) copy-start(bf16[2,64,1024]{2,1,0:T(8,128)(2,1)} %copy-done.5) | copy-start | bytes 786436

commit v2 on v1

--- a/solution.py
+++ b/solution.py
@@ -237,14 +237,16 @@
     )(*operands)
 
 
-def finish_kernel(value_ref, expo_ref, sum_ref, acc_ref, out_ref, rows_ref, sem):
+def finish_kernel(value_ref, expo_ref, before_ref, top_ref, sum_ref, acc_ref, out_ref, rows_ref, sem):
     tok = rows_ref.shape[0]
     width = rows_ref.shape[1] // OUT_PARTS
     copies = []
     for head in range(HEADS):
         cols = pl.ds(head * HEAD_DIM, HEAD_DIM)
-        mixed = weighted(value_ref[:, cols], expo_ref[pl.ds(head * tok, tok), :]) + acc_ref[cols, :]
-        mixed = mixed * (1.0 / sum_ref[pl.ds(head, 1), :])
+        row = pl.ds(head, 1)
+        keep = jnp.exp2(before_ref[row, :] - top_ref[row, :])
+        mixed = weighted(value_ref[:, cols], expo_ref[pl.ds(head * tok, tok), :]) * keep
+        mixed = (mixed + acc_ref[cols, :]) * (1.0 / sum_ref[row, :])
         rows_ref[:, cols] = mixed.T.astype(jnp.bfloat16)
         if (head + 1) * OUT_PARTS % HEADS == 0:
             part = (head + 1) * OUT_PARTS // HEADS - 1
@@ -257,12 +259,12 @@
         copy.wait()
 
 
-def finish(values, expo, total, mixed):
+def finish(values, expo, before, top, total, mixed):
     tok, width = values.shape
     return pl.pallas_call(
         finish_kernel,
         out_shape=jax.ShapeDtypeStruct((tok, width), jnp.bfloat16),
-        in_specs=[pl.BlockSpec(memory_space=pltpu.VMEM)] * 4,
+        in_specs=[pl.BlockSpec(memory_space=pltpu.VMEM)] * 6,
         out_specs=pl.BlockSpec(memory_space=pltpu.HBM),
         scratch_shapes=[
             pltpu.VMEM((tok, width), jnp.bfloat16),
@@ -273,7 +275,7 @@
         cost_estimate=pl.CostEstimate(
             flops=2 * tok * tok * width, bytes_accessed=10 * tok * width, transcendentals=0
         ),
-    )(values, expo, total, mixed)
+    )(values, expo, before, top, total, mixed)
 
 
 def swap(x, axis, mask):
@@ -314,7 +316,7 @@
     one_next = swap(own_one, "seqb", 2)
     other_three = swap(own_three, "seqb", 4)
     chips = [(i, i // 2 % CHIPS_ONE) for i in range(wide)]
-    one_end = lax.ppermute(own_one, "seqb", [(i, i ^ 4) for i, chip in chips if chip in (0, 3)])
+    one_end = lax.ppermute(one_next, "seqb", [(i, i ^ 6) for i, chip in chips if chip in (1, 2)])
     across_keys = lax.ppermute(key_rows, AXES, bounds)
     across_values = lax.ppermute(value_rows, AXES, bounds)
     partner = [swap(key_rows, "seqb", 1), swap(value_rows, "seqb", 1)]
@@ -331,9 +333,11 @@
         ("one", swap(one_far, "seqb", 1)),
     ]
     state = stage(flags, query_rows, far, state)
-    wider = [
+    third = [
         ("pick", one_end, one_mid),
         ("pick", swap(one_end, "seqb", 1), swap(one_mid, "seqb", 1)),
+    ]
+    wider = [
         ("three", three),
         ("three", swap(three, "seqb", 1)),
     ]
@@ -346,8 +350,9 @@
         others = spread(four, "seqa", COLUMNS_THREE, tall)[:, four.shape[1] :]
         others = spread(others, "seqa", 1, COLUMNS_THREE)
         wider.append(("far", spread(others, "seqb", 1, wide)))
-    _, total, mixed, expo = stage(flags, query_rows, wider + [("across", across_keys)], state)
-    return finish(across_values, expo, total, mixed)
+    *state, expo = stage(flags, query_rows, wider + [("across", across_keys)], state)
+    top, total, mixed = stage(flags, query_rows, third, state)
+    return finish(across_values, expo, state[0], top, total, mixed)
 
 
 def solution(mesh):

time: 62.8 us -> 65.5 us (1.043)
  the two profiles are of different devices: /device:TPU:1 before, /device:TPU:19 now
where the time goes in v2:
time: 65.5 us; the launch traced here: 65.2 us
  starting transfers between devices  25.7 us (39%)
  waiting for transfers between devices  22.4 us (34%)
  Pallas kernels  14.4 us (22%)
  local copies, waits for them, and re-layouts  2.4 us (4%)
    ppermute x1, waiting for transfers between devices, attend(): lax.ppermute(one_next, 'seqb', [(i, i ^ 6) for i, chip in chips if chip i...  14.3 us
    ppermute x12, starting transfers between devices, swap(): lax.ppermute(x, axis, [(i, i ^ mask) for i in range(lax.axis_size(axis))])  11.3 us
    pallas_call x4, Pallas kernels, stage(): pl.pallas_call(functools.partial(stage_kernel, plan, state is None), out_...  10.7 us
    ppermute x12, waiting for transfers between devices, swap(): lax.ppermute(x, axis, [(i, i ^ mask) for i in range(lax.axis_size(axis))])  8.09 us
    ppermute x1, starting transfers between devices, attend(): across_keys = lax.ppermute(key_rows, AXES, bounds)  7.16 us
    ppermute x1, starting transfers between devices, attend(): lax.ppermute(one_far, 'seqb', [(i, i ^ 2) for i, chip in chips if chip in...  3.4 us
    unnamed x14, local copies, waits for them, and re-layouts  2.4 us
    ppermute x1, starting transfers between devices, attend(): across_values = lax.ppermute(value_rows, AXES, bounds)  1.91 us
  transfers between devices with their start and end apart: 16, of which 2 were waited for; matrix products, arithmetic and copies ran while one was open for 0% of the time, Pallas kernels for 17%

profile of v2, /device:TPU:19, one launch (start us, length us, event | category | flops | bytes accessed | tf_op | source)
XLA Modules:
  0.0 65.2 jit_solution(2180621358632513258)
XLA Ops:
  0.0 1.8 %pool_own.1 = (bf16[2,64,1024]{2,1,0:T(8,128)(2,1)S(1)}, bf16[2,4,1024]{2,1,0:T(4,128)(2,1)S(1)}) custom-call(bf16[256,1024]{1,0:T(8,128)(2,1)} %refs_2_.1, bf16[256,1024]{1,0:T(8,128)(2,1)} %refs_3_.1), custom_call_target="tpu_custom_call" | custom-call | flops 67108864 | bytes 1310720 | tf_op jit(solution)/shard_map/pool_own/pallas_call | solution.py:54
  1.8 1.4 %collective-permute-start.2 = (bf16[2,64,1024]{2,1,0:T(8,128)(2,1)S(1)}, bf16[2,64,1024]{2,1,0:T(8,128)(2,1)S(1)}, u32[]{:S(2)}, u32[]{:S(2)}) collective-permute-start(bf16[2,64,1024]{2,1,0:T(8,128)(2,1)S(1)} %get-tuple-element.21.refs_4_), channel_id=1, source_target_pairs={{0,2},{1,3},{2,0},{3,1},{4,6},{5,7},{6,4},{7,5},{8,10},{9,11},{10,... | collective-permute-start | bytes 786440 | tf_op jit(solution)/shard_map/ppermute | solution.py:282
  3.1 1.0 %collective-permute-start.10 = (bf16[256,1024]{1,0:T(8,128)(2,1)}, bf16[256,1024]{1,0:T(8,128)(2,1)S(1)}, u32[]{:S(2)}, u32[]{:S(2)}) collective-permute-start(bf16[256,1024]{1,0:T(8,128)(2,1)} %refs_2_.1), channel_id=1, source_target_pairs={{0,1},{1,0},{2,3},{3,2},{4,5},{5,4},{6,7},{7,6},{8,9},{9,8},{10,11... | collective-permute-start | bytes 1572872 | tf_op jit(solution)/shard_map/ppermute | solution.py:282
  4.1 2.5 %collective-permute-start.1 = (bf16[2,4,1024]{2,1,0:T(4,128)(2,1)S(1)}, bf16[2,4,1024]{2,1,0:T(4,128)(2,1)S(1)}, u32[]{:S(2)}, u32[]{:S(2)}) collective-permute-start(bf16[2,4,1024]{2,1,0:T(4,128)(2,1)S(1)} %get-tuple-element.20.three_ref), channel_id=1, source_target_pairs={{0,4},{1,5},{2,6},{3,7},{4,0},{5,1},{6,2},{7,3},{8,12},{9,13},{10,... | collective-permute-start | bytes 49160 | tf_op jit(solution)/shard_map/ppermute | solution.py:282
  6.6 8.1 %collective-permute-done.1.other_ref = bf16[2,4,1024]{2,1,0:T(4,128)(2,1)S(1)} collective-permute-done((bf16[2,4,1024]{2,1,0:T(4,128)(2,1)S(1)}, bf16[2,4,1024]{2,1,0:T(4,128)(2,1)S(1)}, u32[]{:S(2)}, u32[]{:S(2)}) %collective-permute-start.1) | collective-permute-done | bytes 16416 | tf_op jit(solution)/shard_map/ppermute | solution.py:282
  14.7 0.7 %lift.1 = bf16[2,16,1024]{2,1,0:T(8,128)(2,1)S(1)} custom-call(bf16[2,4,1024]{2,1,0:T(4,128)(2,1)S(1)} %get-tuple-element.20.three_ref, bf16[2,4,1024]{2,1,0:T(4,128)(2,1)S(1)} %collective-permute-done.1.other_ref, bf16[2,64,1024]{2,1,0:T(8,128)(2,1)S(1)} %collective-permute-done.2.next_ref.refs_2_, ...), custom_call_target="tpu_custom_call" | custom-call | flops 16777216 | bytes 1228800 | tf_op jit(solution)/shard_map/lift/pallas_call | solution.py:82
  15.4 0.3 collective-permute-start.4
  15.7 3.6 %collective-permute-start.8 = (bf16[2,64,1024]{2,1,0:T(8,128)(2,1)S(1)}, bf16[2,64,1024]{2,1,0:T(8,128)(2,1)S(1)}, u32[]{:S(2)}, u32[]{:S(2)}) collective-permute-start(bf16[2,64,1024]{2,1,0:T(8,128)(2,1)S(1)} %collective-permute-done.2.next_ref.refs_2_), channel_id=1, source_target_pairs={{0,1},{1,0},{2,3},{3,2},{4,5},{5,4},{6,7},{7,6},{8,9},{9,8},{10,11... | collective-permute-start | bytes 786440 | tf_op jit(solution)/shard_map/ppermute | solution.py:282
  19.3 1.3 %collective-permute-start.5 = (bf16[2,32,1024]{2,1,0:T(8,128)(2,1)S(1)}, bf16[2,32,1024]{2,1,0:T(8,128)(2,1)S(1)}, u32[]{:S(2)}, u32[]{:S(2)}) collective-permute-start(bf16[2,32,1024]{2,1,0:T(8,128)(2,1)S(1)} %pad_maximum_fusion.1), channel_id=1, source_target_pairs={{0,16},{8,24},{16,0},{24,8},{1,17},{9,25},{17,1},{25,9},{2,18},{10... | collective-permute-start | bytes 393224 | tf_op jit(solution)/shard_map/ppermute | solution.py:282
  20.6 7.2 %collective-permute-start.7 = (bf16[256,1024]{1,0:T(8,128)(2,1)}, bf16[256,1024]{1,0:T(8,128)(2,1)S(1)}, u32[]{:S(2)}, u32[]{:S(2)}) collective-permute-start(bf16[256,1024]{1,0:T(8,128)(2,1)} %refs_2_.1), channel_id=1, source_target_pairs={{1,2},{3,4},{5,6},{7,8},{9,10},{11,12},{13,14},{15,16},{17,18},{19... | collective-permute-start | bytes 1572872 | tf_op jit(solution)/shard_map/ppermute | solution.py:320
  28.1 1.9 %collective-permute-start.12 = (bf16[2,64,1024]{2,1,0:T(8,128)(2,1)S(1)}, bf16[2,64,1024]{2,1,0:T(8,128)(2,1)}, u32[]{:S(2)}, u32[]{:S(2)}) collective-permute-start(bf16[2,64,1024]{2,1,0:T(8,128)(2,1)S(1)} %collective-permute-done.2.next_ref.refs_2_), channel_id=1, source_target_pairs={{2,4},{3,5},{4,2},{5,3},{10,12},{11,13},{12,10},{13,11},{18,20},{1... | collective-permute-start | bytes 786440 | tf_op jit(solution)/shard_map/ppermute | solution.py:319
  30.0 3.4 %collective-permute-start.13 = (bf16[2,64,1024]{2,1,0:T(8,128)(2,1)S(1)}, bf16[2,64,1024]{2,1,0:T(8,128)(2,1)}, u32[]{:S(2)}, u32[]{:S(2)}) collective-permute-start(bf16[2,64,1024]{2,1,0:T(8,128)(2,1)S(1)} %collective-permute-done.3.far_ref.refs_4_), channel_id=1, source_target_pairs={{2,0},{3,1},{4,6},{5,7},{10,8},{11,9},{12,14},{13,15},{18,16},{19,... | collective-permute-start | bytes 786440 | tf_op jit(solution)/shard_map/ppermute | solution.py:325
  33.4 0.7 %copy-done.3 = bf16[2,64,1024]{2,1,0:T(8,128)(2,1)} copy-done((bf16[2,64,1024]{2,1,0:T(8,128)(2,1)}, bf16[2,64,1024]{2,1,0:T(8,128)(2,1)S(1)}, u32[]{:S(2)}) %copy-start.3) | copy-done | bytes 262168
  34.1 1.9 %collective-permute-start = (bf16[256,1024]{1,0:T(8,128)(2,1)}, bf16[256,1024]{1,0:T(8,128)(2,1)S(1)}, u32[]{:S(2)}, u32[]{:S(2)}) collective-permute-start(bf16[256,1024]{1,0:T(8,128)(2,1)} %refs_3_.1), channel_id=1, source_target_pairs={{1,2},{3,4},{5,6},{7,8},{9,10},{11,12},{13,14},{15,16},{17,18},{19... | collective-permute-start | bytes 1572872 | tf_op jit(solution)/shard_map/ppermute | solution.py:321
  36.1 0.7 %copy-done.5 = bf16[2,64,1024]{2,1,0:T(8,128)(2,1)} copy-done((bf16[2,64,1024]{2,1,0:T(8,128)(2,1)}, bf16[2,64,1024]{2,1,0:T(8,128)(2,1)S(1)}, u32[]{:S(2)}) %copy-start.5) | copy-done | bytes 262168
  36.8 0.4 collective-permute-start.6
  37.2 14.3 %collective-permute-done.12.refs_2_ = bf16[2,64,1024]{2,1,0:T(8,128)(2,1)} collective-permute-done((bf16[2,64,1024]{2,1,0:T(8,128)(2,1)S(1)}, bf16[2,64,1024]{2,1,0:T(8,128)(2,1)}, u32[]{:S(2)}, u32[]{:S(2)}) %collective-permute-start.12) | collective-permute-done | bytes 262176 | tf_op jit(solution)/shard_map/ppermute | solution.py:319
  51.6 0.5 collective-permute-start.15
  52.1 0.9 %copy-done.2 = bf16[2,64,1024]{2,1,0:T(8,128)(2,1)S(1)} copy-done((bf16[2,64,1024]{2,1,0:T(8,128)(2,1)S(1)}, bf16[2,64,1024]{2,1,0:T(8,128)(2,1)}, u32[]{:S(2)}) %copy-start.2) | copy-done | bytes 262168
  53.1 4.0 %shard_map.37 = (f32[8,256]{1,0:T(8,128)S(1)}, f32[8,256]{1,0:T(8,128)S(1)}, f32[1024,256]{1,0:T(8,128)S(1)}) custom-call(s32[3]{0:T(128)S(1)} %pad_add_fusion.refs_0_, bf16[256,1024]{1,0:T(8,128)(2,1)S(1)} %copy-done, bf16[256,1024]{1,0:T(8,128)(2,1)} %refs_2_.1, bf16[256,1024]{1,0:T(8,128)(2,1)} %refs_3_.1, bf16[2,64,1024]{2,1,0:T(8,128)(2,1)S(1)} %copy-done.2, ...), custom_call_target="tpu_custom_call" | custom-call | flops 704643072 | bytes 2883596 | tf_op jit(solution)/shard_map/pallas_call | solution.py:222
  57.1 2.1 %shard_map.38 = (f32[8,256]{1,0:T(8,128)S(1)}, f32[8,256]{1,0:T(8,128)S(1)}, f32[1024,256]{1,0:T(8,128)S(1)}) custom-call(s32[3]{0:T(128)S(1)} %pad_add_fusion.refs_0_, bf16[256,1024]{1,0:T(8,128)(2,1)S(1)} %copy-done, bf16[2,64,1024]{2,1,0:T(8,128)(2,1)S(1)} %collective-permute-done.2.next_ref.refs_2_, bf16[2,64,1024]{2,1,0:T(8,128)(2,1)S(1)} %copy-done.4, ...), custom_call_target="tpu_custom_call" | custom-call | flops 335544320 | bytes 2637836 | tf_op jit(solution)/shard_map/pallas_call | solution.py:222
  59.2 2.5 %shard_map.39 = (f32[8,256]{1,0:T(8,128)S(1)}, f32[8,256]{1,0:T(8,128)S(1)}, f32[1024,256]{1,0:T(8,128)S(1)}, bf16[2048,256]{1,0:T(8,128)(2,1)S(1)}) custom-call(s32[3]{0:T(128)S(1)} %pad_add_fusion.refs_0_, bf16[256,1024]{1,0:T(8,128)(2,1)S(1)} %copy-done, bf16[2,64,1024]{2,1,0:T(8,128)(2,1)S(1)} %pad_maximum_fusion.refs_2_, ...), custom_call_target="tpu_custom_call" | custom-call | flops 436207616 | bytes 2637836 | tf_op jit(solution)/shard_map/pallas_call | solution.py:222
  61.8 2.1 %shard_map.40 = (f32[8,256]{1,0:T(8,128)S(1)}, f32[8,256]{1,0:T(8,128)S(1)}, f32[1024,256]{1,0:T(8,128)S(1)}) custom-call(s32[3]{0:T(128)S(1)} %pad_add_fusion.refs_0_, bf16[256,1024]{1,0:T(8,128)(2,1)S(1)} %copy-done, bf16[2,64,1024]{2,1,0:T(8,128)(2,1)} %collective-permute-done.12.refs_2_, bf16[2,64,1024]{2,1,0:T(8,128)(2,1)} %collective-permute-done.13.refs_3_, ...), custom_call_target="tpu_custom_call" | custom-call | flops 167772160 | bytes 2637836 | tf_op jit(solution)/shard_map/pallas_call | solution.py:222
  63.9 1.2 %finish.1 = bf16[256,1024]{1,0:T(8,128)(2,1)} custom-call(bf16[256,1024]{1,0:T(8,128)(2,1)S(1)} %collective-permute-done.value_ref, bf16[2048,256]{1,0:T(8,128)(2,1)S(1)} %get-tuple-element.28.expo_ref, f32[8,256]{1,0:T(8,128)S(1)} %get-tuple-element.29.refs_6_.before_ref, f32[8,256]{1,0:T(8,128)S(1)} %get-tuple-element.32.top_ref, ...), custom_call_target="tpu_custom_call" | custom-call | flops 134217728 | bytes 2621440 | tf_op jit(solution)/shard_map/finish/pallas_call | solution.py:264
  (32 shorter events, 0.5 us)
Async XLA Ops:
  1.8 13.6 %copy-start.1 = (bf16[2,64,1024]{2,1,0:T(8,128)(2,1)}, bf16[2,64,1024]{2,1,0:T(8,128)(2,1)S(1)}, u32[]{:S(2)}) copy-start(bf16[2,64,1024]{2,1,0:T(8,128)(2,1)S(1)} %get-tuple-element.21.refs_4_) | copy-start | bytes 786436
  1.8 12.9 %collective-permute-start.2 = (bf16[2,64,1024]{2,1,0:T(8,128)(2,1)S(1)}, bf16[2,64,1024]{2,1,0:T(8,128)(2,1)S(1)}, u32[]{:S(2)}, u32[]{:S(2)}) collective-permute-start(bf16[2,64,1024]{2,1,0:T(8,128)(2,1)S(1)} %get-tuple-element.21.refs_4_), channel_id=1, source_target_pairs={{0,2},{1,3},{2,0},{3,1},{4,6},{5,7},{6,4},{7,5},{8,10},{9,11},{10,... | collective-permute-start | bytes 786440 | tf_op jit(solution)/shard_map/ppermute | solution.py:282
  3.1 11.6 %collective-permute-start.3 = (bf16[2,64,1024]{2,1,0:T(8,128)(2,1)S(1)}, bf16[2,64,1024]{2,1,0:T(8,128)(2,1)S(1)}, u32[]{:S(2)}, u32[]{:S(2)}) collective-permute-start(bf16[2,64,1024]{2,1,0:T(8,128)(2,1)S(1)} %get-tuple-element.21.refs_4_), channel_id=1, source_target_pairs={{0,6},{1,7},{2,4},{3,5},{4,2},{5,3},{6,0},{7,1},{8,14},{9,15},{10,... | collective-permute-start | bytes 786440 | tf_op jit(solution)/shard_map/ppermute | solution.py:282
  3.1 24.9 %collective-permute-start.10 = (bf16[256,1024]{1,0:T(8,128)(2,1)}, bf16[256,1024]{1,0:T(8,128)(2,1)S(1)}, u32[]{:S(2)}, u32[]{:S(2)}) collective-permute-start(bf16[256,1024]{1,0:T(8,128)(2,1)} %refs_2_.1), channel_id=1, source_target_pairs={{0,1},{1,0},{2,3},{3,2},{4,5},{5,4},{6,7},{7,6},{8,9},{9,8},{10,11... | collective-permute-start | bytes 1572872 | tf_op jit(solution)/shard_map/ppermute | solution.py:282
  4.1 25.9 %collective-permute-start.11 = (bf16[256,1024]{1,0:T(8,128)(2,1)}, bf16[256,1024]{1,0:T(8,128)(2,1)S(1)}, u32[]{:S(2)}, u32[]{:S(2)}) collective-permute-start(bf16[256,1024]{1,0:T(8,128)(2,1)} %refs_3_.1), channel_id=1, source_target_pairs={{0,1},{1,0},{2,3},{3,2},{4,5},{5,4},{6,7},{7,6},{8,9},{9,8},{10,11... | collective-permute-start | bytes 1572872 | tf_op jit(solution)/shard_map/ppermute | solution.py:282
  4.1 10.6 %collective-permute-start.1 = (bf16[2,4,1024]{2,1,0:T(4,128)(2,1)S(1)}, bf16[2,4,1024]{2,1,0:T(4,128)(2,1)S(1)}, u32[]{:S(2)}, u32[]{:S(2)}) collective-permute-start(bf16[2,4,1024]{2,1,0:T(4,128)(2,1)S(1)} %get-tuple-element.20.three_ref), channel_id=1, source_target_pairs={{0,4},{1,5},{2,6},{3,7},{4,0},{5,1},{6,2},{7,3},{8,12},{9,13},{10,... | collective-permute-start | bytes 49160 | tf_op jit(solution)/shard_map/ppermute | solution.py:282
  15.4 36.8 %copy-start = (bf16[256,1024]{1,0:T(8,128)(2,1)S(1)}, bf16[256,1024]{1,0:T(8,128)(2,1)}, u32[]{:S(2)}) copy-start(bf16[256,1024]{1,0:T(8,128)(2,1)} %refs_1_.7) | copy-start | bytes 1572868
  15.4 3.9 %collective-permute-start.4 = (bf16[2,16,1024]{2,1,0:T(8,128)(2,1)S(1)}, bf16[2,16,1024]{2,1,0:T(8,128)(2,1)S(1)}, u32[]{:S(2)}, u32[]{:S(2)}) collective-permute-start(bf16[2,16,1024]{2,1,0:T(8,128)(2,1)S(1)} %lift.1), channel_id=1, source_target_pairs={{0,8},{8,0},{16,24},{24,16},{1,9},{9,1},{17,25},{25,17},{2,10},{10... | collective-permute-start | bytes 196616 | tf_op jit(solution)/shard_map/ppermute | solution.py:282
  15.7 17.7 %collective-permute-start.8 = (bf16[2,64,1024]{2,1,0:T(8,128)(2,1)S(1)}, bf16[2,64,1024]{2,1,0:T(8,128)(2,1)S(1)}, u32[]{:S(2)}, u32[]{:S(2)}) collective-permute-start(bf16[2,64,1024]{2,1,0:T(8,128)(2,1)S(1)} %collective-permute-done.2.next_ref.refs_2_), channel_id=1, source_target_pairs={{0,1},{1,0},{2,3},{3,2},{4,5},{5,4},{6,7},{7,6},{8,9},{9,8},{10,11... | collective-permute-start | bytes 786440 | tf_op jit(solution)/shard_map/ppermute | solution.py:282
  19.3 8.5 %collective-permute-start.5 = (bf16[2,32,1024]{2,1,0:T(8,128)(2,1)S(1)}, bf16[2,32,1024]{2,1,0:T(8,128)(2,1)S(1)}, u32[]{:S(2)}, u32[]{:S(2)}) collective-permute-start(bf16[2,32,1024]{2,1,0:T(8,128)(2,1)S(1)} %pad_maximum_fusion.1), channel_id=1, source_target_pairs={{0,16},{8,24},{16,0},{24,8},{1,17},{9,25},{17,1},{25,9},{2,18},{10... | collective-permute-start | bytes 393224 | tf_op jit(solution)/shard_map/ppermute | solution.py:282
  20.6 38.6 %collective-permute-start.7 = (bf16[256,1024]{1,0:T(8,128)(2,1)}, bf16[256,1024]{1,0:T(8,128)(2,1)S(1)}, u32[]{:S(2)}, u32[]{:S(2)}) collective-permute-start(bf16[256,1024]{1,0:T(8,128)(2,1)} %refs_2_.1), channel_id=1, source_target_pairs={{1,2},{3,4},{5,6},{7,8},{9,10},{11,12},{13,14},{15,16},{17,18},{19... | collective-permute-start | bytes 1572872 | tf_op jit(solution)/shard_map/ppermute | solution.py:320
  27.8 8.3 %collective-permute-start.9 = (bf16[2,64,1024]{2,1,0:T(8,128)(2,1)S(1)}, bf16[2,64,1024]{2,1,0:T(8,128)(2,1)S(1)}, u32[]{:S(2)}, u32[]{:S(2)}) collective-permute-start(bf16[2,64,1024]{2,1,0:T(8,128)(2,1)S(1)} %collective-permute-done.3.far_ref.refs_4_), channel_id=1, source_target_pairs={{0,1},{1,0},{2,3},{3,2},{4,5},{5,4},{6,7},{7,6},{8,9},{9,8},{10,11... | collective-permute-start | bytes 786440 | tf_op jit(solution)/shard_map/ppermute | solution.py:282
  28.1 23.5 %collective-permute-start.12 = (bf16[2,64,1024]{2,1,0:T(8,128)(2,1)S(1)}, bf16[2,64,1024]{2,1,0:T(8,128)(2,1)}, u32[]{:S(2)}, u32[]{:S(2)}) collective-permute-start(bf16[2,64,1024]{2,1,0:T(8,128)(2,1)S(1)} %collective-permute-done.2.next_ref.refs_2_), channel_id=1, source_target_pairs={{2,4},{3,5},{4,2},{5,3},{10,12},{11,13},{12,10},{13,11},{18,20},{1... | collective-permute-start | bytes 786440 | tf_op jit(solution)/shard_map/ppermute | solution.py:319
  30.0 21.6 %collective-permute-start.13 = (bf16[2,64,1024]{2,1,0:T(8,128)(2,1)S(1)}, bf16[2,64,1024]{2,1,0:T(8,128)(2,1)}, u32[]{:S(2)}, u32[]{:S(2)}) collective-permute-start(bf16[2,64,1024]{2,1,0:T(8,128)(2,1)S(1)} %collective-permute-done.3.far_ref.refs_4_), channel_id=1, source_target_pairs={{2,0},{3,1},{4,6},{5,7},{10,8},{11,9},{12,14},{13,15},{18,16},{19,... | collective-permute-start | bytes 786440 | tf_op jit(solution)/shard_map/ppermute | solution.py:325
  33.4 0.7 %copy-start.3 = (bf16[2,64,1024]{2,1,0:T(8,128)(2,1)}, bf16[2,64,1024]{2,1,0:T(8,128)(2,1)S(1)}, u32[]{:S(2)}) copy-start(bf16[2,64,1024]{2,1,0:T(8,128)(2,1)S(1)} %collective-permute-done.8.refs_3_) | copy-start | bytes 786436
  34.1 29.8 %collective-permute-start = (bf16[256,1024]{1,0:T(8,128)(2,1)}, bf16[256,1024]{1,0:T(8,128)(2,1)S(1)}, u32[]{:S(2)}, u32[]{:S(2)}) collective-permute-start(bf16[256,1024]{1,0:T(8,128)(2,1)} %refs_3_.1), channel_id=1, source_target_pairs={{1,2},{3,4},{5,6},{7,8},{9,10},{11,12},{13,14},{15,16},{17,18},{19... | collective-permute-start | bytes 1572872 | tf_op jit(solution)/shard_map/ppermute | solution.py:321
  36.1 0.7 %copy-start.5 = (bf16[2,64,1024]{2,1,0:T(8,128)(2,1)}, bf16[2,64,1024]{2,1,0:T(8,128)(2,1)S(1)}, u32[]{:S(2)}) copy-start(bf16[2,64,1024]{2,1,0:T(8,128)(2,1)S(1)} %collective-permute-done.9.refs_5_) | copy-start | bytes 786436
  36.8 22.5 %collective-permute-start.6 = (bf16[2,64,1024]{2,1,0:T(8,128)(2,1)S(1)}, bf16[2,64,1024]{2,1,0:T(8,128)(2,1)}, u32[]{:S(2)}, u32[]{:S(2)}) collective-permute-start(bf16[2,64,1024]{2,1,0:T(8,128)(2,1)S(1)} %pad_maximum_fusion.refs_2_), channel_id=1, source_target_pairs={{0,1},{1,0},{2,3},{3,2},{4,5},{5,4},{6,7},{7,6},{8,9},{9,8},{10,11... | collective-permute-start | bytes 786440 | tf_op jit(solution)/shard_map/ppermute | solution.py:282
  51.6 10.2 %collective-permute-start.14 = (bf16[2,64,1024]{2,1,0:T(8,128)(2,1)}, bf16[2,64,1024]{2,1,0:T(8,128)(2,1)}, u32[]{:S(2)}, u32[]{:S(2)}) collective-permute-start(bf16[2,64,1024]{2,1,0:T(8,128)(2,1)} %collective-permute-done.12.refs_2_), channel_id=1, source_target_pairs={{0,1},{1,0},{2,3},{3,2},{4,5},{5,4},{6,7},{7,6},{8,9},{9,8},{10,11... | collective-permute-start | bytes 786440 | tf_op jit(solution)/shard_map/ppermute | solution.py:282
  51.6 10.2 %collective-permute-start.15 = (bf16[2,64,1024]{2,1,0:T(8,128)(2,1)}, bf16[2,64,1024]{2,1,0:T(8,128)(2,1)}, u32[]{:S(2)}, u32[]{:S(2)}) collective-permute-start(bf16[2,64,1024]{2,1,0:T(8,128)(2,1)} %collective-permute-done.13.refs_3_), channel_id=1, source_target_pairs={{0,1},{1,0},{2,3},{3,2},{4,5},{5,4},{6,7},{7,6},{8,9},{9,8},{10,11... | collective-permute-start | bytes 786440 | tf_op jit(solution)/shard_map/ppermute | solution.py:282
  52.1 1.0 %copy-start.2 = (bf16[2,64,1024]{2,1,0:T(8,128)(2,1)S(1)}, bf16[2,64,1024]{2,1,0:T(8,128)(2,1)}, u32[]{:S(2)}) copy-start(bf16[2,64,1024]{2,1,0:T(8,128)(2,1)} %copy-done.1) | copy-start | bytes 786436
  53.1 4.0 %copy-start.4 = (bf16[2,64,1024]{2,1,0:T(8,128)(2,1)S(1)}, bf16[2,64,1024]{2,1,0:T(8,128)(2,1)}, u32[]{:S(2)}) copy-start(bf16[2,64,1024]{2,1,0:T(8,128)(2,1)} %copy-done.3) | copy-start | bytes 786436
  53.1 4.0 %copy-start.6 = (bf16[2,64,1024]{2,1,0:T(8,128)(2,1)S(1)}, bf16[2,64,1024]{2,1,0:T(8,128)(2,1)}, u32[]{:S(2)}) copy-start(bf16[2,64,1024]{2,1,0:T(8,128)(2,1)} %copy-done.5) | copy-start | bytes 786436
